TPU v7x, 128 devices: a whole 4x4x4 slice. The times are simulated.
128 devices in a mesh: row: 8 (over x_hi, z), rep: 16 (over x_lo, y, core).
Axes of the slice: x: 4 (x_hi: 2, x_lo: 2; x = x_hi * 2 + x_lo), y: 4, z: 4, core: 2. Of those that a mesh axis runs over, the one named last changes fastest.
Arguments:
- features: bfloat16 [32768, 256], P('row'), may hold values from 0 to 2
- self_weight: bfloat16 [256, 256], replicated, may hold values from -0.375 to 0.375
- neigh_weight: bfloat16 [256, 256], replicated, may hold values from -0.375 to 0.375
- out_bias: float32 [256], replicated, may hold values from -4 to 4
- tile_masks: int32 [32768, 128, 128], P('row', 'rep'), may hold values 0 or 1
- tile_live: int32 [256, 128], P('row', 'rep'), may hold values from 0 to 1, as said below
- tile_columns: int32 [256, 128], P('row', 'rep'), may hold values from 0 to 1
- node_degree: int32 [32768], P(('row', 'rep')), may hold values from 128 to 511
- cotangent: bfloat16 [32768, 256], P(('row', 'rep')), may hold values from -6 to 6
Outputs:
- hidden_out: bfloat16 [32768, 256], P(('row', 'rep'))
- grad_features: bfloat16 [32768, 256], P(('row', 'rep'))
- grad_self: float32 [256, 256], replicated
- grad_neigh: float32 [256, 256], replicated
- grad_bias: float32 [256], replicated
Inputs may be any that keep to these rules, and one draw needn't show every extreme that they name: `tile_masks`: an edge bit; bits of slots without a tile are not read. `tile_live`: 1 where the slot holds a tile. `tile_columns`: the covered block among the 2 blocks of that column set and panel.
All inputs are finite; a program needn't handle non-finite values. No bound on the sum of `tile_masks` on one device may be relied on, other than what follows from the above.
Results may differ from a plain program's by a relative error of at most 0.0053.
Values may be sent and summed in bfloat16 or wider, within the bound.
A program may use at most 128 MiB of HBM per device.

v0:
```python
import math

import jax
import jax.numpy as jnp
from jax import lax
from jax.sharding import PartitionSpec as P


def activation(values):
    return jax.nn.gelu(values, approximate=True)


def per_device(
    features,
    self_weight,
    neigh_weight,
    out_bias,
    tile_masks,
    tile_live,
    tile_columns,
    node_degree,
    cotangent,
):
    row_devices = lax.axis_size("row")
    rep_devices = lax.axis_size("rep")
    panel_rows, width = features.shape
    share_rows = node_degree.shape[0]
    panel_count = tile_masks.shape[1]
    tile_size = tile_masks.shape[2]
    block_rows = panel_rows // tile_size
    set_blocks = share_rows // tile_size
    column_rows = panel_count * share_rows
    contract_first = (((0,), (0,)), ((), ()))
    contract_second = (((1,), (1,)), ((), ()))
    block_ids = jnp.arange(set_blocks, dtype=jnp.int32)
    selected = (tile_columns[:, :, None] == block_ids[None, None, :]) & (tile_live[:, :, None] != 0)
    keeper = selected.astype(jnp.bfloat16)
    dense = tile_masks.reshape(block_rows, tile_size, panel_count, 1, tile_size).astype(
        jnp.bfloat16
    )
    dense = (dense * keeper[:, None, :, :, None]).reshape(panel_rows, column_rows)
    own = lax.dynamic_slice_in_dim(features, lax.axis_index("rep") * share_rows, share_rows, 0)
    strip = dense
    partial_sums = jnp.dot(
        strip, lax.all_gather(own, "row", axis=0, tiled=True), preferred_element_type=jnp.float32
    )
    agg_sum = lax.psum_scatter(partial_sums, "rep", scatter_dimension=0, tiled=True)
    degree = node_degree.astype(jnp.float32)[:, None]
    mean = (agg_sum / degree).astype(jnp.bfloat16)
    pre = (
        jnp.dot(own, self_weight, preferred_element_type=jnp.float32)
        + jnp.dot(mean, neigh_weight, preferred_element_type=jnp.float32)
        + out_bias
    )
    result, pull = jax.vjp(activation, pre)
    hidden_out = result.astype(jnp.bfloat16)
    dpre = pull(cotangent.astype(jnp.float32))[0]
    dpre_b = dpre.astype(jnp.bfloat16)
    scale = 1.0 / math.sqrt(share_rows * row_devices * rep_devices)
    self_term = (
        lax.dot_general(own, dpre_b, contract_first, preferred_element_type=jnp.float32) * scale
    )
    neigh_term = (
        lax.dot_general(mean, dpre_b, contract_first, preferred_element_type=jnp.float32) * scale
    )
    bias_term = jnp.sum(dpre, axis=0) * scale
    grad_self, grad_neigh, grad_bias = lax.psum((self_term, neigh_term, bias_term), ("row", "rep"))
    message = (
        lax.dot_general(dpre_b, neigh_weight, contract_second, preferred_element_type=jnp.float32)
        / degree
    ).astype(jnp.bfloat16)
    direct = lax.dot_general(
        dpre_b, self_weight, contract_second, preferred_element_type=jnp.float32
    )
    strip = dense
    partial_back = lax.dot_general(
        strip,
        lax.all_gather(message, "rep", axis=0, tiled=True),
        contract_first,
        preferred_element_type=jnp.float32,
    )
    spread = lax.psum_scatter(
        partial_back.astype(jnp.bfloat16), "row", scatter_dimension=0, tiled=True
    ).astype(jnp.float32)
    grad_features = (direct + spread).astype(jnp.bfloat16)
    return (hidden_out, grad_features, grad_self, grad_neigh, grad_bias)


def solution(mesh):
    return jax.shard_map(
        per_device,
        mesh=mesh,
        in_specs=(
            P("row", None),
            P(),
            P(),
            P(),
            P("row", "rep", None),
            P("row", "rep"),
            P("row", "rep"),
            P(("row", "rep")),
            P(("row", "rep"), None),
        ),
        out_specs=(P(("row", "rep"), None), P(("row", "rep"), None), P(), P(), P()),
        check_vma=False,
    )
```

profile of v0, /device:TPU:1, one launch (start us, length us, event | category | flops | bytes accessed | tf_op | source)
XLA Modules:
  0.0 428.5 jit_solution(4350122207436884132)
XLA Ops:
  7.2 0.0 copy-start
  7.2 0.0 all-gather.3.cloned.1.call-start
  7.2 1.5 copy-done
  8.8 0.7 constant_dynamic-slice_fusion
  9.4 0.0 all-gather.3.cloned.1.call-update
  9.5 0.0 reduce-scatter.3.cloned.1.call-start
  9.5 0.8 copy.14
  10.3 0.7 broadcast_compare_fusion
  11.0 0.1 copy.15
  11.1 6.3 %convert_element_type.45 = bf16[4096,8,128]{2,1,0:T(8,128)(2,1)S(1)} convert(s32[4096,8,128]{2,1,0:T(8,128)} %param.13) | non-fusion elementwise | flops 4194304 | bytes 25165824 | tf_op jit(solution)/shard_map/convert_element_type | solution.py:38
  17.4 0.1 fusion.13
  17.5 19.8 %broadcast_multiply_fusion = bf16[32,128,8,2,128]{4,3,2,1,0:T(2,128)(2,1)} fusion(bf16[32,8,2]{2,1,0:T(8,128)(2,1)S(1)} %fusion.13, bf16[32,128,8,128]{3,2,1,0:T(8,128)(2,1)S(1)} %bitcast.15), kind=kLoop, calls=%fused_computation | loop fusion | flops 8388608 | bytes 25166848 | tf_op jit(solution)/shard_map/mul | solution.py:41
  37.3 27.8 %mul.80 = bf16[4096,2048]{1,0:T(8,128)(2,1)} reshape(bf16[32,128,8,2,128]{4,3,2,1,0:T(2,128)(2,1)} %broadcast_multiply_fusion) | data formatting | bytes 33554432 | tf_op jit(solution)/shard_map/mul | solution.py:41
  65.1 0.0 copy-start.4
  65.1 0.0 copy-start.2
  65.1 0.0 copy-start.3
  65.1 0.0 copy-start.6
  65.1 0.0 copy-start.7
  65.1 0.0 copy-start.8
  65.1 0.0 all-gather.3.cloned.1.call-done
  65.2 12.6 %fusion.17 = f32[4096,256]{1,0:T(8,128)} fusion(bf16[4096,2048]{1,0:T(8,128)(2,1)} %mul.80, bf16[2048,256]{1,0:T(8,128)(2,1)} %all-gather.3.cloned.1.call-done), kind=kOutput, calls=%fused_computation.33 | convolution fusion | flops 4294967296 | bytes 22020096 | tf_op jit(solution)/shard_map/dot_general | solution.py:44
  77.8 0.0 reduce-scatter.3.cloned.1.call-update
  77.8 0.0 all-gather.5.cloned.1.call-start
  77.8 0.0 copy-done.4
  77.9 0.0 copy-done.2
  77.9 0.0 copy-done.3
  77.9 0.2 fusion.16
  78.1 66.0 %reduce-scatter.3.cloned.1.call-done = f32[256,256]{1,0:T(8,128)} async-done(((f32[4096,256]{1,0:T(8,128)}), f32[256,256]{1,0:T(8,128)}) %reduce-scatter.3.cloned.1.call-update) | async-done | bytes 262160 | tf_op jit(solution)/shard_map/reduce_scatter | solution.py:47
  144.1 0.0 copy-done.6
  144.1 0.0 copy-done.7
  144.1 0.0 copy-done.8
  144.1 2.0 fusion.14
  146.1 0.9 fusion.2
  147.0 0.0 all-gather.5.cloned.1.call-update
  147.0 0.0 copy-start.5
  147.0 0.0 copy-start.1
  147.0 0.2 reduce-scatter.5.cloned.1.call-start
  147.3 36.9 %all-gather.5.cloned.1.call-done = bf16[4096,256]{1,0:T(8,128)(2,1)} async-done(((bf16[256,256]{1,0:T(8,128)(2,1)}), bf16[4096,256]{1,0:T(8,128)(2,1)}) %all-gather.5.cloned.1.call-update) | async-done | bytes 2097168 | tf_op jit(solution)/shard_map/all_gather | solution.py:78
  184.1 12.3 %convolution_convert_fusion = bf16[2048,256]{1,0:T(8,128)(2,1)} fusion(bf16[4096,2048]{1,0:T(8,128)(2,1)} %mul.80, bf16[4096,256]{1,0:T(8,128)(2,1)} %all-gather.5.cloned.1.call-done), kind=kOutput, calls=%fused_computation.1 | convolution fusion | flops 4295491584 | bytes 19922944 | tf_op jit(solution)/shard_map/dot_general | solution.py:76
  196.4 0.0 reduce-scatter.5.cloned.1.call-update
  196.4 0.0 all-reduce.3.cloned.1.call-start
  196.5 0.9 convolution_multiply_fusion.1
  197.4 0.0 copy-done.5
  197.4 1.0 convolution_multiply_fusion
  198.4 0.0 all-reduce.3.cloned.1.call-update
  198.5 66.0 %psum.23 = f32[256]{0:T(256)} all-reduce(f32[256]{0:T(256)S(1)} %broadcast_multiply_fusion.1), channel_id=1, replica_groups=mesh['row'=8,'rep'=16] {'row','rep'}, use_global_device_ids=true, to_apply=%region_5.0 | all-reduce | flops 256 | bytes 2048 | tf_op jit(solution)/shard_map/psum | solution.py:67
  264.4 1.8 reduce-scatter.5.cloned.1.call-done
  266.2 1.8 fusion.1
  268.0 150.7 %all-reduce.3.cloned.1.call-done = (f32[256,256]{1,0:T(8,128)}, f32[256,256]{1,0:T(8,128)}) async-done(((f32[256,256]{1,0:T(8,128)}, f32[256,256]{1,0:T(8,128)}), (f32[256,256]{1,0:T(8,128)}, f32[256,256]{1,0:T(8,128)})) %all-reduce.3.cloned.1.call-update) | async-done | bytes 524304 | tf_op jit(solution)/shard_map/psum | solution.py:67
  418.6 1.7 copy.18
  420.3 1.7 copy.19
  422.0 0.0 copy-done.1
  (2 shorter events, 0.0 us)
Async XLA Ops:
  7.2 1.6 copy-start
  7.2 58.0 %all-gather.3.cloned.1.call-start = ((), (), s32[]{:S(2)}) async-start(), calls=%async_computation.2 | async-start | bytes 1179648 | tf_op jit(solution)/shard_map/all_gather | solution.py:45
  9.5 134.6 %reduce-scatter.3.cloned.1.call-start = ((), (), s32[]{:S(2)}) async-start(), calls=%async_computation.3 | async-start | bytes 4456448 | tf_op jit(solution)/shard_map/reduce_scatter | solution.py:47
  65.1 12.7 %copy-start.4 = (s32[256]{0:T(256)S(1)}, s32[256]{0:T(256)}, u32[]{:S(2)}) copy-start(s32[256]{0:T(256)} %param.16) | copy-start | bytes 3076
  65.1 12.8 %copy-start.2 = (bf16[256,256]{1,0:T(8,128)(2,1)S(1)}, bf16[256,256]{1,0:T(8,128)(2,1)}, u32[]{:S(2)}) copy-start(bf16[256,256]{1,0:T(8,128)(2,1)} %constant_dynamic-slice_fusion) | copy-start | bytes 393220
  65.1 12.8 %copy-start.3 = (bf16[256,256]{1,0:T(8,128)(2,1)S(1)}, bf16[256,256]{1,0:T(8,128)(2,1)}, u32[]{:S(2)}) copy-start(bf16[256,256]{1,0:T(8,128)(2,1)} %param.10) | copy-start | bytes 393220
  65.1 79.0 %copy-start.6 = (bf16[256,256]{1,0:T(8,128)(2,1)S(1)}, bf16[256,256]{1,0:T(8,128)(2,1)}, u32[]{:S(2)}) copy-start(bf16[256,256]{1,0:T(8,128)(2,1)} %param.17) | copy-start | bytes 393220
  65.1 78.9 %copy-start.7 = (bf16[256,256]{1,0:T(8,128)(2,1)S(1)}, bf16[256,256]{1,0:T(8,128)(2,1)}, u32[]{:S(2)}) copy-start(bf16[256,256]{1,0:T(8,128)(2,1)} %param.11) | copy-start | bytes 393220
  65.1 78.9 %copy-start.8 = (f32[256]{0:T(256)S(1)}, f32[256]{0:T(256)}, u32[]{:S(2)}) copy-start(f32[256]{0:T(256)} %param.12) | copy-start | bytes 3076
  77.8 106.3 %all-gather.5.cloned.1.call-start = ((), (), s32[]{:S(2)}) async-start(), calls=%async_computation.4 | async-start | bytes 2228224 | tf_op jit(solution)/shard_map/all_gather | solution.py:78
  147.0 50.4 %copy-start.5 = (f32[256,256]{1,0:T(8,128)S(1)}, f32[256,256]{1,0:T(8,128)}, u32[]{:S(2)}) copy-start(f32[256,256]{1,0:T(8,128)} %reduce-scatter.3.cloned.1.call-done) | copy-start | bytes 786436
  147.0 274.9 %copy-start.1 = (bf16[4096,256]{1,0:T(8,128)(2,1)S(1)}, bf16[4096,256]{1,0:T(8,128)(2,1)}, u32[]{:S(2)}) copy-start(bf16[4096,256]{1,0:T(8,128)(2,1)} %param.9) | copy-start | bytes 6291460
  147.0 119.2 %reduce-scatter.5.cloned.1.call-start = ((), (), s32[]{:S(2)}) async-start(), calls=%async_computation.5 | async-start | bytes 1179648 | tf_op jit(solution)/shard_map/reduce_scatter | solution.py:82
  196.4 222.2 %all-reduce.3.cloned.1.call-start = ((), (), s32[]{:S(2)}) async-start(), calls=%async_computation.6 | async-start | bytes 1048576 | tf_op jit(solution)/shard_map/psum | solution.py:67
Sparse Core Ops, SparseCore 0:
  11.0 48.4 all-gather.2
  77.9 66.0 reduce-scatter.2
  147.1 36.9 all-gather.4
  196.6 69.5 reduce-scatter.4
  272.3 146.2 all-reduce.2
where the time goes:
time: 430 us; the launch traced here: 429 us
  waiting for transfers between devices  255 us (59%)
  blocking collectives  66 us (15%)
  local copies, waits for them, and re-layouts  34.2 us (8%)
  matrix products  31.7 us (7%)
  other arithmetic  27 us (6%)
  between operations  13.9 us (3%)
    psum x1, waiting for transfers between devices, per_device(): lax.psum((self_term, neigh_term, bias_term), ('row', 'rep'))  151 us
    reduce_scatter x1, waiting for transfers between devices, per_device(): lax.psum_scatter(partial_sums, 'rep', scatter_dimension=0, tiled=True)  66 us
    psum x1, blocking collectives, per_device(): lax.psum((self_term, neigh_term, bias_term), ('row', 'rep'))  66 us
    all_gather x1, waiting for transfers between devices, per_device(): lax.all_gather(message, 'rep', axis=0, tiled=True)  36.9 us
    mul x1, local copies, waits for them, and re-layouts, per_device(): dense * keeper[:, None, :, :, None]  27.8 us
    mul x1, other arithmetic, per_device(): dense * keeper[:, None, :, :, None]  19.8 us
    dot_general x1, matrix products, per_device(): jnp.dot(strip, lax.all_gather(own, 'row', axis=0, tiled=True), preferred_...  12.6 us
    dot_general x1, matrix products, per_device(): lax.dot_general(strip, lax.all_gather(message, 'rep', axis=0, tiled=True)...  12.3 us
  transfers between devices with their start and end apart: 5, of which 4 were waited for; matrix products, arithmetic and copies ran while one was open for 14% of the time, Pallas kernels for 0%

commit v1 on v0

v1 whole, which is shorter than its diff:
```python
import functools
import math

import jax
import jax.numpy as jnp
from jax import lax
from jax.experimental import pallas as pl
from jax.experimental.pallas import tpu as pltpu
from jax.sharding import PartitionSpec as P

BF = jnp.bfloat16
F32 = jnp.float32
BUFFERS = 4
CONTRACT_LAST = (((1,), (1,)), ((), ()))
CONTRACT_FIRST = (((0,), (0,)), ((), ()))


def kernel(
    rows_n,
    reps_n,
    scale,
    features,
    self_weight,
    neigh_weight,
    bias,
    masks,
    live,
    column,
    degree,
    cotangent,
    hidden_out,
    grad_features,
    grad_self,
    grad_neigh,
    grad_bias,
    dense,
    mask_buf,
    gathered,
    sw_v,
    nw_v,
    bias_v,
    degree_v,
    cot_v,
    own_acc,
    pair_send,
    pair_recv,
    part_send,
    part_recv,
    agg,
    msg,
    msg_recv,
    msg_sib,
    back,
    direct,
    back_send,
    back_recv,
    g1_send,
    g1_recv,
    g1_sum,
    g2_send,
    g2_recv,
    g3,
    g4,
    hid_v,
    gf_v,
    gs_v,
    gn_v,
    gb_v,
    mask_sem,
    in_sem,
    out_sem,
    s1,
    r1,
    s2p,
    r2p,
    s2,
    r2,
    s3,
    r3,
    s3f,
    r3f,
    s4,
    r4,
    sg1,
    rg1,
    sg2,
    rg2,
    sg3,
    rg3,
    sg4,
    rg4,
):
    width = self_weight.shape[0]
    share = cotangent.shape[0]
    tile = masks.shape[1]
    half_rows = rows_n // 2
    chips = reps_n // 2
    mask_rows = tile * rows_n
    blocks = masks.shape[0] // mask_rows
    slot_width = share
    row = lax.axis_index("row")
    rep = lax.axis_index("rep")
    core = rep % 2
    chip = rep // 2
    sibling = chip * 2 + 1 - core
    far_rep = (rep + reps_n // 2) % reps_n

    def remote(src, dst, send, recv, to_row, to_rep):
        return pltpu.make_async_remote_copy(
            src_ref=src,
            dst_ref=dst,
            send_sem=send,
            recv_sem=recv,
            device_id=(to_row, to_rep),
            device_id_type=pl.DeviceIdType.MESH,
        )

    def mask_copy(block, slot):
        return pltpu.make_async_copy(
            masks.at[pl.ds(block * mask_rows, mask_rows), :], mask_buf.at[slot], mask_sem.at[slot]
        )

    for block in range(BUFFERS):
        mask_copy(block, block).start()
    inputs = [
        pltpu.make_async_copy(src, dst, in_sem.at[index])
        for index, (src, dst) in enumerate(
            (
                (self_weight, sw_v),
                (neigh_weight, nw_v),
                (bias, bias_v),
                (degree, degree_v),
                (cotangent, cot_v),
                (
                    features.at[pl.ds(rep * share, share), :],
                    gathered.at[pl.ds(row * share, share), :],
                ),
            )
        )
    ]

    def row_at(far, step):
        return ((row // half_rows + far) % 2) * half_rows + (row % half_rows + step) % half_rows

    row_steps = [
        (far, step) for step in range(half_rows) for far in range(2) if (far, step) != (0, 0)
    ]

    def greet(to_row, to_rep):
        pl.semaphore_signal(
            barrier, inc=1, device_id=(to_row, to_rep), device_id_type=pl.DeviceIdType.MESH
        )

    barrier = pltpu.get_barrier_semaphore()
    greeted = 0
    for step in range(1, reps_n):
        greet(row, (rep + step) % reps_n)
        greeted += 1
    for far, step in row_steps:
        greet(row_at(far, step), rep)
        greeted += 1
        if far:
            greet(row_at(far, step), far_rep)
            greeted += 1
    pl.semaphore_wait(barrier, greeted)

    def feature_copy(far, step):
        to_rep = far_rep if far else rep
        return remote(
            features.at[pl.ds(to_rep * share, share), :],
            gathered.at[pl.ds(row * share, share), :],
            s1.at[far * half_rows + step],
            r1.at[far * half_rows + step],
            row_at(far, step),
            to_rep,
        )

    for far, step in row_steps:
        feature_copy(far, step).start()
    for copy in inputs:
        copy.start()

    def expand(block, carry):
        slot = block % BUFFERS
        mask_copy(block, slot).wait()
        at = pl.ds(pl.multiple_of(block * tile, tile), tile)
        for s in range(rows_n):
            bits = mask_buf[slot, pl.ds(s, tile, stride=rows_n), :].astype(F32)
            held = live[s, block].astype(F32)
            second = held * column[s, block].astype(F32)
            first = held - second
            dense[at, s * slot_width : s * slot_width + tile] = (bits * first).astype(BF)
            dense[at, s * slot_width + tile : (s + 1) * slot_width] = (bits * second).astype(BF)

        @pl.when(block + BUFFERS < blocks)
        def _():
            mask_copy(block + BUFFERS, slot).start()

        return carry

    lax.fori_loop(0, blocks, expand, 0)
    for copy in inputs:
        copy.wait()
    for far, step in row_steps:
        feature_copy(far, step).wait_recv()

    def share_rows(index):
        return pl.ds(pl.multiple_of(index * share, share), share)

    def pair_copy(t):
        return remote(pair_send.at[t], pair_recv.at[t], s2p.at[t], r2p.at[t], row, sibling)

    def part_copy(t):
        return remote(
            part_send.at[t],
            part_recv.at[t],
            s2.at[t],
            r2.at[t],
            row,
            ((chip + 1 + t) % chips) * 2 + core,
        )

    def finish_pair(t):
        pair_copy(t).wait_recv()
        part_send[t] = (own_acc[t % 2] + pair_recv[t].astype(F32)).astype(BF)
        part_copy(t).start()

    def forward(t, carry):
        at = (chip + 1 + t) % chips
        pair_send[t] = jnp.dot(
            dense[share_rows(at * 2 + 1 - core), :], gathered[...], preferred_element_type=F32
        ).astype(BF)
        pair_copy(t).start()

        own_acc[t % 2] = jnp.dot(
            dense[share_rows(at * 2 + core), :], gathered[...], preferred_element_type=F32
        )

        @pl.when(t > 0)
        def _():
            finish_pair(t - 1)

        return carry

    lax.fori_loop(0, chips, forward, 0)
    pair_copy(chips - 1).wait_recv()
    agg[...] = own_acc[(chips - 1) % 2] + pair_recv[chips - 1].astype(F32)
    own = gathered[share_rows(row), :]
    pre_own = jnp.dot(own, sw_v[...], preferred_element_type=F32) + bias_v[...]
    direct[...] = pre_own
    degree_row = degree_v[...].astype(F32)
    degree_column = jnp.transpose(jnp.broadcast_to(degree_row, (width, share)))
    for t in range(chips - 1):
        part_copy(t).wait_recv()
        agg[...] += part_recv[t].astype(F32)

    mean = (agg[...] / degree_column).astype(BF)
    pre = direct[...] + jnp.dot(mean, nw_v[...], preferred_element_type=F32)
    root = math.sqrt(2.0 / math.pi)
    square = pre * pre
    bend = jnp.tanh(root * (pre + 0.044715 * (square * pre)))
    hid_v[...] = (0.5 * pre * (1.0 + bend)).astype(BF)
    slope = 0.5 * (1.0 + bend) + (0.5 * root) * pre * (1.0 - bend * bend) * (
        1.0 + (3.0 * 0.044715) * square
    )
    dpre = cot_v[...].astype(F32) * slope
    dpre_b = dpre.astype(BF)
    msg[...] = (
        lax.dot_general(nw_v[...], dpre_b, CONTRACT_LAST, preferred_element_type=F32) / degree_row
    ).astype(BF)

    def msg_copy(t):
        return remote(
            msg, msg_recv.at[t], s3.at[t], r3.at[t], row, ((chip + 1 + t) % chips) * 2 + core
        )

    def sib_copy(src, t):
        return remote(src, msg_sib.at[t], s3f.at[t], r3f.at[t], row, sibling)

    sib_copy(msg, chips - 1).start()
    for t in range(chips - 1):
        msg_copy(t).start()

    outs = [
        pltpu.make_async_copy(src, dst, out_sem.at[index])
        for index, (src, dst) in enumerate(
            (
                (hid_v, hidden_out),
                (gs_v, grad_self),
                (gn_v, grad_neigh),
                (gb_v, grad_bias),
                (gf_v, grad_features),
            )
        )
    ]
    outs[0].start()

    g_rows = 2 * width // rows_n
    lanes = width // 2
    tile_rows = g_rows // (reps_n // 2)
    terms = [
        lax.dot_general(left, dpre_b, CONTRACT_FIRST, preferred_element_type=F32) * scale
        for left in (own, mean)
    ]
    bias_term = jnp.sum(dpre, axis=0, keepdims=True) * scale
    for index in range(rows_n):
        term = terms[index * g_rows // width]
        low = index * g_rows % width
        for side in range(2):
            g1_send[index, side * (reps_n // 2) : (side + 1) * (reps_n // 2)] = term[
                low : low + g_rows, side * lanes : (side + 1) * lanes
            ].reshape(reps_n // 2, tile_rows, lanes)
        for side in range(2):
            g1_send[index, reps_n + side] = jnp.broadcast_to(
                bias_term[:, side * lanes : (side + 1) * lanes], (tile_rows, lanes)
            )

    def g1_copy(far, step):
        index = far * half_rows + step
        to_row = row_at(far, step)
        return remote(
            g1_send.at[to_row], g1_recv.at[index], sg1.at[index], rg1.at[index], to_row, rep
        )

    for far, step in row_steps:
        g1_copy(far, step).start()
    direct[...] = lax.dot_general(sw_v[...], dpre_b, CONTRACT_LAST, preferred_element_type=F32)

    def spread(block, owner, start):
        at = share_rows(owner)
        for s in range(rows_n):
            term = jnp.dot(
                block, dense[at, s * slot_width : (s + 1) * slot_width], preferred_element_type=F32
            )
            if start:
                back[s] = term
            else:
                back[s] += term

    def backward(t, carry):
        source = (chip + chips - 1 - t) % chips
        msg_copy(t).wait_recv()
        sib_copy(msg_recv.at[t], t).start()
        spread(msg_recv[t], source * 2 + core, False)
        sib_copy(msg_recv.at[t], t).wait_recv()
        spread(msg_sib[t], source * 2 + 1 - core, False)
        return carry

    spread(msg[...], rep, True)
    sib_copy(msg, chips - 1).wait_recv()
    spread(msg_sib[chips - 1], sibling, False)
    lax.fori_loop(0, chips - 1, backward, 0)

    def back_copy(far, step):
        index = far * half_rows + step
        return remote(
            back_send.at[index],
            back_recv.at[index],
            s4.at[index],
            r4.at[index],
            row_at(far, step),
            rep,
        )

    for far, step in row_steps:
        back_send[far * half_rows + step] = back[row_at(far, step)].astype(BF)
        back_copy(far, step).start()

    total = g1_send[row]
    for far, step in row_steps:
        g1_copy(far, step).wait_recv()
        total = total + g1_recv[far * half_rows + step]
    g1_sum[...] = total
    for index in range(reps_n):
        g2_send[index, 0] = g1_sum[index]
        g2_send[index, 1] = g1_sum[reps_n]
        g2_send[index, 2] = g1_sum[reps_n + 1]

    def g2_copy(step):
        to_rep = (rep + step) % reps_n
        return remote(g2_send.at[to_rep], g2_recv.at[step], sg2.at[step], rg2.at[step], row, to_rep)

    for step in range(1, reps_n):
        g2_copy(step).start()
    total = g2_send[rep]
    for step in range(1, reps_n):
        g2_copy(step).wait_recv()
        total = total + g2_recv[step]
    g3[row] = total[0]
    for side in range(2):
        gb_v[:, side * lanes : (side + 1) * lanes] = total[1 + side][0:1, :]
    outs[3].start()

    def g3_copy(far, step):
        index = far * half_rows + step
        return remote(
            g3.at[row], g3.at[row], sg3.at[index], rg3.at[index], row_at(far, step), rep
        )

    for far, step in row_steps:
        g3_copy(far, step).start()
    for far, step in row_steps:
        g3_copy(far, step).wait_recv()

    def g4_copy(step):
        return remote(
            g3, g4.at[rep], sg4.at[step], rg4.at[step], row, (rep + step) % reps_n
        )

    for step in range(1, reps_n):
        g4_copy(step).start()
    g4[rep] = g3[...]
    for step in range(1, reps_n):
        g4_copy(step).wait_recv()
    for index in range(rows_n):
        out = (gs_v, gn_v)[index * g_rows // width]
        low = index * g_rows % width
        for side in range(2):
            out[low : low + g_rows, side * lanes : (side + 1) * lanes] = g4[
                side * (reps_n // 2) : (side + 1) * (reps_n // 2), index
            ].reshape(g_rows, lanes)
    outs[1].start()
    outs[2].start()

    direct[...] += back[row]
    for far, step in row_steps:
        back_copy(far, step).wait_recv()
        direct[...] += back_recv[far * half_rows + step].astype(F32)
    gf_v[...] = jnp.transpose(direct[...]).astype(BF)
    outs[4].start()

    for far, step in row_steps:
        feature_copy(far, step).wait_send()
        g1_copy(far, step).wait_send()
        back_copy(far, step).wait_send()
        g3_copy(far, step).wait_send()
    for t in range(chips):
        pair_copy(t).wait_send()
    for t in range(chips - 1):
        part_copy(t).wait_send()
        msg_copy(t).wait_send()
        sib_copy(msg_recv.at[t], t).wait_send()
    sib_copy(msg, chips - 1).wait_send()
    for step in range(1, reps_n):
        g2_copy(step).wait_send()
        g4_copy(step).wait_send()
    for copy in outs:
        copy.wait()


def per_device(
    features,
    self_weight,
    neigh_weight,
    out_bias,
    tile_masks,
    tile_live,
    tile_columns,
    node_degree,
    cotangent,
):
    rows_n = lax.axis_size("row")
    reps_n = lax.axis_size("rep")
    panel_rows, width = features.shape
    share = node_degree.shape[0]
    slots = tile_masks.shape[1]
    tile = tile_masks.shape[2]
    chips = reps_n // 2
    lanes = width // 2
    tile_rows = 2 * width // rows_n // (reps_n // 2)
    scale = 1.0 / math.sqrt(share * rows_n * reps_n)
    block = (share, width)
    anywhere = pl.BlockSpec(memory_space=pl.ANY)
    scalars = pl.BlockSpec(memory_space=pltpu.SMEM)
    dma = pltpu.SemaphoreType.DMA
    vmem = pltpu.VMEM
    grads = (reps_n + 2, tile_rows, lanes)
    scratch = [
        vmem((panel_rows, slots * share), BF),
        vmem((BUFFERS, tile * slots, tile), jnp.int32),
        vmem((rows_n * share, width), BF),
        vmem((width, width), BF),
        vmem((width, width), BF),
        vmem((1, width), F32),
        vmem((1, share), jnp.int32),
        vmem(block, BF),
        vmem((2, *block), F32),
        vmem((chips, *block), BF),
        vmem((chips, *block), BF),
        vmem((chips, *block), BF),
        vmem((chips, *block), BF),
        vmem(block, F32),
        vmem((width, share), BF),
        vmem((chips, width, share), BF),
        vmem((chips, width, share), BF),
        vmem((rows_n, width, share), F32),
        vmem((width, share), F32),
        vmem((rows_n, width, share), BF),
        vmem((rows_n, width, share), BF),
        vmem((rows_n, *grads), F32),
        vmem((rows_n, *grads), F32),
        vmem(grads, F32),
        vmem((reps_n, 3, tile_rows, lanes), F32),
        vmem((reps_n, 3, tile_rows, lanes), F32),
        vmem((rows_n, tile_rows, lanes), F32),
        vmem((reps_n, rows_n, tile_rows, lanes), F32),
        vmem(block, BF),
        vmem(block, BF),
        vmem((width, width), F32),
        vmem((width, width), F32),
        vmem((1, width), F32),
        dma((BUFFERS,)),
        dma((6,)),
        dma((5,)),
        dma((rows_n,)),
        dma((rows_n,)),
        dma((chips,)),
        dma((chips,)),
        dma((chips,)),
        dma((chips,)),
        dma((chips,)),
        dma((chips,)),
        dma((chips,)),
        dma((chips,)),
        dma((rows_n,)),
        dma((rows_n,)),
        dma((rows_n,)),
        dma((rows_n,)),
        dma((reps_n,)),
        dma((reps_n,)),
        dma((rows_n,)),
        dma((rows_n,)),
        dma((reps_n,)),
        dma((reps_n,)),
    ]
    hidden, grad_features, grad_self, grad_neigh, grad_bias = pl.pallas_call(
        functools.partial(kernel, rows_n, reps_n, scale),
        out_shape=(
            jax.ShapeDtypeStruct(block, BF),
            jax.ShapeDtypeStruct(block, BF),
            jax.ShapeDtypeStruct((width, width), F32),
            jax.ShapeDtypeStruct((width, width), F32),
            jax.ShapeDtypeStruct((1, width), F32),
        ),
        in_specs=[anywhere] * 5 + [scalars] * 2 + [anywhere] * 2,
        out_specs=(anywhere,) * 5,
        scratch_shapes=scratch,
        compiler_params=pltpu.CompilerParams(
            collective_id=0, has_side_effects=True, vmem_limit_bytes=56 * 1024 * 1024
        ),
        name="layer",
    )(
        features,
        self_weight,
        neigh_weight,
        out_bias.reshape(1, width),
        tile_masks.reshape(panel_rows * slots, tile),
        tile_live.T,
        tile_columns.T,
        node_degree.reshape(1, share),
        cotangent,
    )
    return (hidden, grad_features, grad_self, grad_neigh, grad_bias.reshape(width))


def solution(mesh):
    return jax.shard_map(
        per_device,
        mesh=mesh,
        in_specs=(
            P("row", None),
            P(),
            P(),
            P(),
            P("row", "rep", None),
            P("row", "rep"),
            P("row", "rep"),
            P(("row", "rep")),
            P(("row", "rep"), None),
        ),
        out_specs=(P(("row", "rep"), None), P(("row", "rep"), None), P(), P(), P()),
        check_vma=False,
    )
```

time: 430 us -> 105 us (0.24)
  waiting for transfers between devices: 255 us -> 0 us
  Pallas kernels: 0 us -> 95.7 us
  blocking collectives: 66 us -> 0 us
  matrix products: 31.7 us -> 0 us
  other arithmetic: 27 us -> 0 us
  local copies, waits for them, and re-layouts: 34.2 us -> 7.7 us
  between operations: 13.9 us -> 0.64 us
    psum x1 -> x0, waiting for transfers between devices: 151 us -> none  [per_device(): lax.psum((self_term, neigh_term, bias_term), ('row', 'rep'))]
    pallas_call x0 -> x1, Pallas kernels: none -> 95.7 us  [per_device(): pl.pallas_call(functools.partial(kernel, rows_n, reps_n, scale), out_shap...]
    reduce_scatter x2 -> x0, waiting for transfers between devices: 67.7 us -> none  [the longest x1 66 us: per_device(): lax.psum_scatter(partial_sums, 'rep', scatter_dimension=0, tiled=True)]
    psum x1 -> x0, blocking collectives: 66 us -> none  [per_device(): lax.psum((self_term, neigh_term, bias_term), ('row', 'rep'))]
    all_gather x2 -> x0, waiting for transfers between devices: 36.9 us -> none  [the longest x1 36.9 us: per_device(): lax.all_gather(message, 'rep', axis=0, tiled=True)]
    dot_general x8 -> x0, matrix products: 31.7 us -> none  [the longest x1 12.6 us: per_device(): jnp.dot(strip, lax.all_gather(own, 'row', axis=0, tiled=True), preferred_...]
    mul x1 -> x0, local copies, waits for them, and re-layouts: 27.8 us -> none  [per_device(): dense * keeper[:, None, :, :, None]]
    mul x2 -> x0, other arithmetic: 19.8 us -> none  [the longest x1 19.8 us: per_device(): dense * keeper[:, None, :, :, None]]
  transfers between devices with their start and end apart: 5 -> 0, of which waited for: 4 -> 0; matrix products, arithmetic and copies ran while one was open for 14% -> 0% of each run, Pallas kernels for 0% -> 0%
where the time goes in v1:
time: 105 us; the launch traced here: 104 us
  Pallas kernels  95.7 us (91%)
  local copies, waits for them, and re-layouts  7.7 us (7%)
    pallas_call x1, Pallas kernels, per_device(): pl.pallas_call(functools.partial(kernel, rows_n, reps_n, scale), out_shap...  95.7 us
    unnamed x5, local copies, waits for them, and re-layouts  7.7 us

profile of v1, /device:TPU:1, one launch (start us, length us, event | category | flops | bytes accessed | tf_op | source)
XLA Modules:
  0.0 104.1 jit_solution(10981287482354230319)
XLA Ops:
  0.6 95.7 %layer.1 = (bf16[256,256]{1,0:T(8,128)(2,1)}, bf16[256,256]{1,0:T(8,128)(2,1)}, f32[256,256]{1,0:T(8,128)}, f32[256,256]{1,0:T(8,128)}, f32[1,256]{1,0:T(1,128)}) custom-call(bf16[4096,256]{1,0:T(8,128)(2,1)} %features.1, bf16[256,256]{1,0:T(8,128)(2,1)} %self_weight.1, bf16[256,256]{1,0:T(8,128)(2,1)} %neigh_weight.1, f32[1,256]{1,0:T(1,128)} %bitcast.9, ...), custom_call_target="tpu_custom_call" | custom-call | tf_op jit(solution)/shard_map/layer/pallas_call | solution.py:536
  96.4 1.6 %copy.19 = bf16[256,256]{1,0:T(8,128)(2,1)} copy(bf16[256,256]{1,0:T(8,128)(2,1)} %get-tuple-element.20) | data formatting | bytes 262144
  98.0 1.6 %copy.20 = bf16[256,256]{1,0:T(8,128)(2,1)} copy(bf16[256,256]{1,0:T(8,128)(2,1)} %get-tuple-element.21) | data formatting | bytes 262144
  99.5 1.7 %copy.21 = f32[256,256]{1,0:T(8,128)} copy(f32[256,256]{1,0:T(8,128)} %get-tuple-element.22) | data formatting | bytes 524288
  101.2 1.7 %copy.22 = f32[256,256]{1,0:T(8,128)} copy(f32[256,256]{1,0:T(8,128)} %get-tuple-element.23) | data formatting | bytes 524288
  102.9 1.2 %copy.23 = f32[256]{0:T(256)} copy(f32[256]{0:T(256)} %bitcast.11) | data formatting | bytes 2048

commit v2 on v1

v2 whole, which is shorter than its diff:
```python
import functools
import math

import jax
import jax.numpy as jnp
from jax import lax
from jax.experimental import pallas as pl
from jax.experimental.pallas import tpu as pltpu
from jax.sharding import PartitionSpec as P

BF = jnp.bfloat16
F32 = jnp.float32
BUFFERS = 16
CONTRACT_LAST = (((1,), (1,)), ((), ()))
CONTRACT_FIRST = (((0,), (0,)), ((), ()))


def kernel(
    rows_n,
    reps_n,
    scale,
    features,
    self_weight,
    neigh_weight,
    bias,
    masks,
    live,
    column,
    degree,
    cotangent,
    hidden_out,
    grad_features,
    grad_self,
    grad_neigh,
    grad_bias,
    dense,
    mask_buf,
    feat_v,
    gathered,
    sw_v,
    nw_v,
    bias_v,
    degree_v,
    cot_v,
    work,
    pair_send,
    pair_recv,
    part_send,
    part_recv,
    own_sum,
    pre_v,
    mean_v,
    msg_all,
    direct,
    back_own,
    back_send,
    back_recv,
    g1_send,
    g1_recv,
    g1_sum,
    g2_send,
    g2_recv,
    g3,
    g4,
    hid_v,
    gf_v,
    gs_v,
    gn_v,
    gb_v,
    mask_sem,
    in_sem,
    out_sem,
    s1,
    r1,
    s2p,
    r2p,
    s2,
    r2,
    s3,
    r3,
    s3f,
    r3f,
    s4,
    r4,
    sg1,
    rg1,
    sg2,
    rg2,
    sg3,
    rg3,
    sg4,
    rg4,
    sg4f,
    rg4f,
):
    width = self_weight.shape[0]
    share = cotangent.shape[0]
    half = width // 2
    tile = masks.shape[1]
    half_rows = rows_n // 2
    chips = reps_n // 2
    ring = chips // 2
    mask_rows = tile * rows_n
    blocks = masks.shape[0] // mask_rows
    slot_width = share
    row = lax.axis_index("row")
    rep = lax.axis_index("rep")
    core = rep % 2
    chip = rep // 2
    sibling = chip * 2 + 1 - core
    far_rep = (rep + reps_n // 2) % reps_n

    def remote(src, dst, send, recv, to_row, to_rep):
        return pltpu.make_async_remote_copy(
            src_ref=src,
            dst_ref=dst,
            send_sem=send,
            recv_sem=recv,
            device_id=(to_row, to_rep),
            device_id_type=pl.DeviceIdType.MESH,
        )

    def share_rows(index):
        return pl.ds(pl.multiple_of(index * share, share), share)

    def row_at(far, step):
        return ((row // half_rows + far) % 2) * half_rows + (row % half_rows + step) % half_rows

    def chip_at(across, along):
        return ((chip // ring + across) % 2) * ring + (chip % ring + along) % ring

    def chip_from(across, along):
        return ((chip // ring + across) % 2) * ring + (chip % ring + ring - along) % ring

    def offset(t, size):
        across = (t + 1) % 2
        turn = t // 2
        return across, (across * (1 + turn) + (1 - across) * (size - 1 - turn)) % size

    row_steps = [
        (far, step) for step in range(half_rows) for far in range(2) if (far, step) != (0, 0)
    ]

    def mask_copy(block, slot):
        return pltpu.make_async_copy(
            masks.at[pl.ds(pl.multiple_of(block * mask_rows, mask_rows), mask_rows), :],
            mask_buf.at[slot],
            mask_sem.at[slot],
        )

    def greet(to_row, to_rep):
        pl.semaphore_signal(
            barrier, inc=1, device_id=(to_row, to_rep), device_id_type=pl.DeviceIdType.MESH
        )

    barrier = pltpu.get_barrier_semaphore()
    greeted = 0
    for far, step in row_steps:
        greet(row_at(far, step), rep)
        greeted += 1
        if far:
            greet(row_at(far, step), far_rep)
            greeted += 1
    for step in range(1, reps_n):
        greet(row, (rep + step) % reps_n)
        greeted += 1

    inputs = [
        pltpu.make_async_copy(src, dst, in_sem.at[index])
        for index, (src, dst) in enumerate(
            (
                (features.at[share_rows(rep), :], feat_v.at[0]),
                (features.at[share_rows(far_rep), :], feat_v.at[1]),
                (self_weight, sw_v),
                (neigh_weight, nw_v),
                (bias, bias_v),
                (degree, degree_v),
                (cotangent, cot_v),
            )
        )
    ]
    inputs[0].start()
    inputs[1].start()
    for block in range(BUFFERS):
        mask_copy(block, block).start()
    for copy in inputs[2:]:
        copy.start()

    def expand(block, carry):
        slot = block % BUFFERS
        mask_copy(block, slot).wait()
        at = pl.ds(pl.multiple_of(block * tile, tile), tile)
        for s in range(rows_n):
            bits = mask_buf[slot, pl.ds(s, tile, stride=rows_n), :].astype(F32)
            held = live[s, block].astype(F32)
            second = held * column[s, block].astype(F32)
            first = held - second
            dense[at, s * slot_width : s * slot_width + tile] = (bits * first).astype(BF)
            dense[at, s * slot_width + tile : (s + 1) * slot_width] = (bits * second).astype(BF)

        @pl.when(block + BUFFERS < blocks)
        def _():
            mask_copy(block + BUFFERS, slot).start()

        return carry

    def feature_copy(part, far, step):
        return remote(
            feat_v.at[far, :, part * half : (part + 1) * half],
            gathered.at[part, share_rows(row), :],
            s1.at[part, far * half_rows + step],
            r1.at[part, far * half_rows + step],
            row_at(far, step),
            far_rep if far else rep,
        )

    lax.fori_loop(0, blocks // 2, expand, 0)
    inputs[0].wait()
    inputs[1].wait()
    pl.semaphore_wait(barrier, greeted)
    for far, step in row_steps:
        feature_copy(0, far, step).start()
    lax.fori_loop(blocks // 2, blocks, expand, 0)
    for copy in inputs[2:]:
        copy.wait()
    for part in range(2):
        gathered[part, share_rows(row), :] = feat_v[0, :, part * half : (part + 1) * half]
    own = feat_v[0]
    pre_v[...] = jnp.dot(own, sw_v[...], preferred_element_type=F32) + bias_v[...]
    degree_row = degree_v[...].astype(F32)
    degree_column = jnp.transpose(jnp.broadcast_to(degree_row, (half, share)))
    for far, step in row_steps:
        feature_copy(0, far, step).wait_send()
    for far, step in row_steps:
        feature_copy(1, far, step).start()

    def pair_copy(part, t):
        return remote(
            pair_send.at[part, t],
            pair_recv.at[part, t],
            s2p.at[part, t],
            r2p.at[part, t],
            row,
            sibling,
        )

    def part_copy(part, t):
        return remote(
            part_send.at[part, t],
            part_recv.at[part, t],
            s2.at[part, t],
            r2.at[part, t],
            row,
            chip_at(*offset(t, ring)) * 2 + core,
        )

    def finish_pair(part, t):
        pair_copy(part, t).wait_recv()
        part_send[part, t] = (work[t % 2, core] + pair_recv[part, t].astype(F32)).astype(BF)
        part_copy(part, t).start()

    def forward(part):
        def body(t, carry):
            at = chip_at(*offset(t, ring))
            rows = pl.ds(pl.multiple_of(at * (2 * share), 2 * share), 2 * share)
            work[t % 2] = jnp.dot(
                dense[rows, :], gathered[part], preferred_element_type=F32
            ).reshape(2, share, half)
            pair_send[part, t] = work[t % 2, 1 - core].astype(BF)
            pair_copy(part, t).start()

            @pl.when(t > 0)
            def _():
                finish_pair(part, t - 1)

            return carry

        for far, step in row_steps:
            feature_copy(part, far, step).wait_recv()
        lax.fori_loop(0, chips, body, 0)
        pair_copy(part, chips - 1).wait_recv()
        own_sum[part] = work[(chips - 1) % 2, core] + pair_recv[part, chips - 1].astype(F32)

    forward(0)
    forward(1)
    for part in range(2):
        total = own_sum[part]
        for t in range(chips - 1):
            part_copy(part, t).wait_recv()
            total = total + part_recv[part, t].astype(F32)
        mean = (total / degree_column).astype(BF)
        mean_v[:, part * half : (part + 1) * half] = mean
        pre_v[...] += jnp.dot(
            mean, nw_v[part * half : (part + 1) * half, :], preferred_element_type=F32
        )

    pre = pre_v[...]
    root = math.sqrt(2.0 / math.pi)
    square = pre * pre
    bend = jnp.tanh(root * (pre + 0.044715 * (square * pre)))
    slope = 0.5 * (1.0 + bend) + (0.5 * root) * pre * (1.0 - bend * bend) * (
        1.0 + (3.0 * 0.044715) * square
    )
    dpre = cot_v[...].astype(F32) * slope
    dpre_b = dpre.astype(BF)

    def message_copy(part, across, along):
        relay = across and along
        source = (chip_at(1, 0) if relay else chip) * 2 + core
        place = msg_all.at[part, :, share_rows(source)]
        index = across * ring + along
        target = chip_at(0 if relay else across, along) * 2 + core
        return remote(place, place, s3.at[part, index], r3.at[part, index], row, target)

    def sibling_copy(part, across, along):
        place = msg_all.at[part, :, share_rows(chip_from(across, along) * 2 + core)]
        index = across * ring + along
        return remote(place, place, s3f.at[part, index], r3f.at[part, index], row, sibling)

    along_order = sorted(range(1, ring), key=lambda d: min(d, ring - d))

    def send_messages(part):
        message_copy(part, 1, 0).start()
        for along in along_order:
            message_copy(part, 0, along).start()
        sibling_copy(part, 0, 0).start()

    def relay_messages(part):
        message_copy(part, 1, 0).wait_recv()
        for along in along_order:
            message_copy(part, 1, along).start()
        sibling_copy(part, 1, 0).start()

    def finish_messages(part):
        for across in range(2):
            for along in along_order:
                message_copy(part, across, along).wait_recv()
                sibling_copy(part, across, along).start()
        for across in range(2):
            for along in range(ring):
                sibling_copy(part, across, along).wait_recv()

    for part in range(2):
        msg_all[part, :, share_rows(rep)] = (
            lax.dot_general(
                nw_v[part * half : (part + 1) * half, :],
                dpre_b,
                CONTRACT_LAST,
                preferred_element_type=F32,
            )
            / degree_row
        ).astype(BF)
        if part == 0:
            send_messages(0)

    outs = [
        pltpu.make_async_copy(src, dst, out_sem.at[index])
        for index, (src, dst) in enumerate(
            (
                (hid_v, hidden_out),
                (gs_v, grad_self),
                (gn_v, grad_neigh),
                (gb_v, grad_bias),
                (gf_v, grad_features),
            )
        )
    ]
    hid_v[...] = (0.5 * pre * (1.0 + bend)).astype(BF)
    outs[0].start()

    g_rows = 2 * width // rows_n
    tile_rows = g_rows // (reps_n // 2)
    terms = [
        lax.dot_general(left, dpre_b, CONTRACT_FIRST, preferred_element_type=F32) * scale
        for left in (feat_v[0], mean_v[...])
    ]
    bias_term = jnp.sum(dpre, axis=0, keepdims=True) * scale
    for index in range(rows_n):
        term = terms[index * g_rows // width]
        low = index * g_rows % width
        for side in range(2):
            g1_send[index, side * (reps_n // 2) : (side + 1) * (reps_n // 2)] = term[
                low : low + g_rows, side * half : (side + 1) * half
            ].reshape(reps_n // 2, tile_rows, half)
            g1_send[index, reps_n + side] = jnp.broadcast_to(
                bias_term[:, side * half : (side + 1) * half], (tile_rows, half)
            )

    def g1_copy(far, step):
        index = far * half_rows + step
        to_row = row_at(far, step)
        return remote(
            g1_send.at[to_row],
            g1_recv.at[index],
            sg1.at[index],
            rg1.at[index],
            to_row,
            far_rep if far else rep,
        )

    for far, step in row_steps:
        g1_copy(far, step).start()
    direct[...] = lax.dot_general(
        sw_v[...], dpre_b, CONTRACT_LAST, preferred_element_type=F32
    ).reshape(2, half, share)

    def back_copy(part, t):
        return remote(
            back_send.at[part, t],
            back_recv.at[part, t],
            s4.at[part, t],
            r4.at[part, t],
            row_at(*offset(t, half_rows)),
            rep,
        )

    def backward(part):
        def body(t, carry):
            target = row_at(*offset(t, half_rows))
            columns = pl.ds(pl.multiple_of(target * slot_width, slot_width), slot_width)
            term = jnp.dot(msg_all[part], dense[:, columns], preferred_element_type=F32)

            @pl.when(t < rows_n - 1)
            def _():
                back_send[part, t] = term.astype(BF)
                back_copy(part, t).start()

            @pl.when(t == rows_n - 1)
            def _():
                back_own[part] = term

            return carry

        lax.fori_loop(0, rows_n, body, 0)

    relay_messages(0)
    finish_messages(0)
    send_messages(1)
    backward(0)

    def g2_copy(step):
        to_rep = (rep + step) % reps_n
        return remote(g2_send.at[to_rep], g2_recv.at[step], sg2.at[step], rg2.at[step], row, to_rep)

    def g3_copy(far, step):
        index = far * half_rows + step
        return remote(g3.at[row], g3.at[row], sg3.at[index], rg3.at[index], row_at(far, step), rep)

    def g4_copy(t):
        return remote(
            g3, g4.at[rep], sg4.at[t], rg4.at[t], row, chip_at(*offset(t, ring)) * 2 + core
        )

    def g4_pair(t):
        source = chip_from(*offset(t, ring)) * 2 + core
        return remote(g4.at[source], g4.at[source], sg4f.at[t], rg4f.at[t], row, sibling)

    relay_messages(1)
    total = g1_send[row]
    for far, step in row_steps:
        g1_copy(far, step).wait_recv()
        total = total + g1_recv[far * half_rows + step]
    g1_sum[...] = total
    for index in range(reps_n):
        g2_send[index, 0] = g1_sum[index]
        g2_send[index, 1] = g1_sum[reps_n]
        g2_send[index, 2] = g1_sum[reps_n + 1]
    for step in range(1, reps_n):
        g2_copy(step).start()

    finish_messages(1)
    backward(1)

    total = g2_send[rep]
    for step in range(1, reps_n):
        g2_copy(step).wait_recv()
        total = total + g2_recv[step]
    g3[row] = total[0]
    for far, step in row_steps:
        g3_copy(far, step).start()
    for side in range(2):
        gb_v[:, side * half : (side + 1) * half] = total[1 + side][0:1, :]
    outs[3].start()

    def column_sums(part):
        total = direct[part] + back_own[part]
        for t in range(rows_n - 1):
            back_copy(part, t).wait_recv()
            total = total + back_recv[part, t].astype(F32)
        gf_v[:, part * half : (part + 1) * half] = jnp.transpose(total).astype(BF)

    column_sums(0)
    for far, step in row_steps:
        g3_copy(far, step).wait_recv()
    for t in range(chips - 1):
        g4_copy(t).start()
    g4[rep] = g3[...]
    g4_pair(chips - 1).start()
    for t in range(chips - 1):
        g4_copy(t).wait_recv()
        g4_pair(t).start()
    for t in range(chips):
        g4_pair(t).wait_recv()
    for index in range(rows_n):
        out = (gs_v, gn_v)[index * g_rows // width]
        low = index * g_rows % width
        for side in range(2):
            out[low : low + g_rows, side * half : (side + 1) * half] = g4[
                side * (reps_n // 2) : (side + 1) * (reps_n // 2), index
            ].reshape(g_rows, half)
    outs[1].start()
    outs[2].start()
    column_sums(1)
    outs[4].start()

    for far, step in row_steps:
        feature_copy(1, far, step).wait_send()
        g1_copy(far, step).wait_send()
        g3_copy(far, step).wait_send()
    for part in range(2):
        for t in range(chips):
            pair_copy(part, t).wait_send()
        for t in range(chips - 1):
            part_copy(part, t).wait_send()
        for t in range(rows_n - 1):
            back_copy(part, t).wait_send()
        for across in range(2):
            for along in range(ring):
                if across or along:
                    message_copy(part, across, along).wait_send()
                sibling_copy(part, across, along).wait_send()
    for step in range(1, reps_n):
        g2_copy(step).wait_send()
    for t in range(chips):
        if t < chips - 1:
            g4_copy(t).wait_send()
        g4_pair(t).wait_send()
    for copy in outs:
        copy.wait()


def store(*refs):
    count = len(refs) // 2
    sems = refs[-1]
    copies = [
        pltpu.make_async_copy(refs[index], refs[count + index], sems.at[index])
        for index in range(count)
    ]
    for copy in copies:
        copy.start()
    for copy in copies:
        copy.wait()


def per_device(
    features,
    self_weight,
    neigh_weight,
    out_bias,
    tile_masks,
    tile_live,
    tile_columns,
    node_degree,
    cotangent,
):
    rows_n = lax.axis_size("row")
    reps_n = lax.axis_size("rep")
    panel_rows, width = features.shape
    share = node_degree.shape[0]
    slots = tile_masks.shape[1]
    tile = tile_masks.shape[2]
    chips = reps_n // 2
    lanes = width // 2
    tile_rows = 2 * width // rows_n // (reps_n // 2)
    scale = 1.0 / math.sqrt(share * rows_n * reps_n)
    block = (share, width)
    anywhere = pl.BlockSpec(memory_space=pl.ANY)
    scalars = pl.BlockSpec(memory_space=pltpu.SMEM)
    dma = pltpu.SemaphoreType.DMA
    vmem = pltpu.VMEM
    grads = (reps_n + 2, tile_rows, lanes)
    half_block = (share, lanes)
    turned = (lanes, share)
    scratch = [
        vmem((panel_rows, slots * share), BF),
        vmem((BUFFERS, tile * slots, tile), jnp.int32),
        vmem((2, *block), BF),
        vmem((2, rows_n * share, lanes), BF),
        vmem((width, width), BF),
        vmem((width, width), BF),
        vmem((1, width), F32),
        vmem((1, share), jnp.int32),
        vmem(block, BF),
        vmem((2, 2, *half_block), F32),
        vmem((2, chips, *half_block), BF),
        vmem((2, chips, *half_block), BF),
        vmem((2, chips, *half_block), BF),
        vmem((2, chips, *half_block), BF),
        vmem((2, *half_block), F32),
        vmem(block, F32),
        vmem(block, BF),
        vmem((2, lanes, panel_rows), BF),
        vmem((2, *turned), F32),
        vmem((2, *turned), F32),
        vmem((2, rows_n, *turned), BF),
        vmem((2, rows_n, *turned), BF),
        vmem((rows_n, *grads), F32),
        vmem((rows_n, *grads), F32),
        vmem(grads, F32),
        vmem((reps_n, 3, tile_rows, lanes), F32),
        vmem((reps_n, 3, tile_rows, lanes), F32),
        vmem((rows_n, tile_rows, lanes), F32),
        vmem((reps_n, rows_n, tile_rows, lanes), F32),
        vmem(block, BF),
        vmem(block, BF),
        vmem((width, width), F32),
        vmem((width, width), F32),
        vmem((1, width), F32),
        dma((BUFFERS,)),
        dma((7,)),
        dma((5,)),
        dma((2, rows_n)),
        dma((2, rows_n)),
    ]
    scratch += [dma((2, chips))] * 8 + [dma((2, rows_n))] * 2 + [dma((rows_n,))] * 2
    scratch += [dma((reps_n,))] * 2 + [dma((rows_n,))] * 2 + [dma((chips,))] * 4
    results = pl.pallas_call(
        functools.partial(kernel, rows_n, reps_n, scale),
        out_shape=(
            jax.ShapeDtypeStruct(block, BF),
            jax.ShapeDtypeStruct(block, BF),
            jax.ShapeDtypeStruct((width, width), F32),
            jax.ShapeDtypeStruct((width, width), F32),
            jax.ShapeDtypeStruct((1, width), F32),
        ),
        in_specs=[anywhere] * 5 + [scalars] * 2 + [anywhere] * 2,
        out_specs=(anywhere,) * 5,
        scratch_shapes=scratch,
        compiler_params=pltpu.CompilerParams(
            collective_id=0, has_side_effects=True, vmem_limit_bytes=56 * 1024 * 1024
        ),
        name="layer",
    )(
        features,
        self_weight,
        neigh_weight,
        out_bias.reshape(1, width),
        tile_masks.reshape(panel_rows * slots, tile),
        tile_live.T,
        tile_columns.T,
        node_degree.reshape(1, share),
        cotangent,
    )
    hidden, grad_features, grad_self, grad_neigh, grad_bias = pl.pallas_call(
        store,
        out_shape=tuple(jax.ShapeDtypeStruct(one.shape, one.dtype) for one in results),
        in_specs=[anywhere] * 5,
        out_specs=(anywhere,) * 5,
        scratch_shapes=[dma((5,))],
        name="store",
    )(*results)
    return (hidden, grad_features, grad_self, grad_neigh, grad_bias.reshape(width))


def solution(mesh):
    return jax.shard_map(
        per_device,
        mesh=mesh,
        in_specs=(
            P("row", None),
            P(),
            P(),
            P(),
            P("row", "rep", None),
            P("row", "rep"),
            P("row", "rep"),
            P(("row", "rep")),
            P(("row", "rep"), None),
        ),
        out_specs=(P(("row", "rep"), None), P(("row", "rep"), None), P(), P(), P()),
        check_vma=False,
    )
```

time: 105 us -> 105 us (level)
  Pallas kernels: 95.7 us -> 104 us
  local copies, waits for them, and re-layouts: 7.7 us -> 0 us
    pallas_call x0 -> x1, Pallas kernels: none -> 25 us  [per_device(): pl.pallas_call(store, out_shape=tuple((jax.ShapeDtypeStruct(one.shape, on...]
    pallas_call x1, Pallas kernels: 95.7 us -> 78.8 us  [per_device(): pl.pallas_call(functools.partial(kernel, rows_n, reps_n, scale), out_shap...]
    unnamed x5 -> x0, local copies, waits for them, and re-layouts: 7.7 us -> none
where the time goes in v2:
time: 105 us; the launch traced here: 104 us
  Pallas kernels  104 us (99%)
    pallas_call x1, Pallas kernels, per_device(): pl.pallas_call(functools.partial(kernel, rows_n, reps_n, scale), out_shap...  78.8 us
    pallas_call x1, Pallas kernels, per_device(): pl.pallas_call(store, out_shape=tuple((jax.ShapeDtypeStruct(one.shape, on...  25 us

profile of v2, /device:TPU:1, one launch (start us, length us, event | category | flops | bytes accessed | tf_op | source)
XLA Modules:
  0.0 104.5 jit_solution(13663305086959839250)
XLA Ops:
  0.6 78.8 %layer.1 = (bf16[256,256]{1,0:T(8,128)(2,1)}, bf16[256,256]{1,0:T(8,128)(2,1)}, f32[256,256]{1,0:T(8,128)}, f32[256,256]{1,0:T(8,128)}, f32[1,256]{1,0:T(1,128)}) custom-call(bf16[4096,256]{1,0:T(8,128)(2,1)} %features.1, bf16[256,256]{1,0:T(8,128)(2,1)} %self_weight.1, bf16[256,256]{1,0:T(8,128)(2,1)} %neigh_weight.1, f32[1,256]{1,0:T(1,128)} %bitcast.9, ...), custom_call_target="tpu_custom_call" | custom-call | tf_op jit(solution)/shard_map/layer/pallas_call | solution.py:627
  79.5 25.0 %store.1 = (bf16[256,256]{1,0:T(8,128)(2,1)}, bf16[256,256]{1,0:T(8,128)(2,1)}, f32[256,256]{1,0:T(8,128)}, f32[256,256]{1,0:T(8,128)}, f32[1,256]{1,0:T(1,128)}) custom-call(bf16[256,256]{1,0:T(8,128)(2,1)} %get-tuple-element.15.refs_0_, bf16[256,256]{1,0:T(8,128)(2,1)} %get-tuple-element.16.refs_1_, f32[256,256]{1,0:T(8,128)} %get-tuple-element.17.refs_2_, ...), custom_call_target="tpu_custom_call" | custom-call | tf_op jit(solution)/shard_map/store/pallas_call | solution.py:654

commit v3 on v2

--- a/solution.py
+++ b/solution.py
@@ -11,6 +11,7 @@
 BF = jnp.bfloat16
 F32 = jnp.float32
 BUFFERS = 16
+LAG = 2
 CONTRACT_LAST = (((1,), (1,)), ((), ()))
 CONTRACT_FIRST = (((0,), (0,)), ((), ()))
 
@@ -24,8 +25,8 @@
     neigh_weight,
     bias,
     masks,
-    live,
-    column,
+    live_hbm,
+    column_hbm,
     degree,
     cotangent,
     hidden_out,
@@ -33,6 +34,8 @@
     grad_self,
     grad_neigh,
     grad_bias,
+    live,
+    column,
     dense,
     mask_buf,
     feat_v,
@@ -105,10 +108,12 @@
     slot_width = share
     row = lax.axis_index("row")
     rep = lax.axis_index("rep")
-    core = rep % 2
-    chip = rep // 2
+    core = lax.rem(rep, 2)
+    chip = lax.div(rep, 2)
+    row_far, row_step = lax.div(row, half_rows), lax.rem(row, half_rows)
+    chip_across, chip_along = lax.div(chip, ring), lax.rem(chip, ring)
     sibling = chip * 2 + 1 - core
-    far_rep = (rep + reps_n // 2) % reps_n
+    far_rep = lax.rem(rep + reps_n // 2, reps_n)
 
     def remote(src, dst, send, recv, to_row, to_rep):
         return pltpu.make_async_remote_copy(
@@ -124,18 +129,20 @@
         return pl.ds(pl.multiple_of(index * share, share), share)
 
     def row_at(far, step):
-        return ((row // half_rows + far) % 2) * half_rows + (row % half_rows + step) % half_rows
+        return lax.rem(row_far + far, 2) * half_rows + lax.rem(row_step + step, half_rows)
 
     def chip_at(across, along):
-        return ((chip // ring + across) % 2) * ring + (chip % ring + along) % ring
+        return lax.rem(chip_across + across, 2) * ring + lax.rem(chip_along + along, ring)
 
     def chip_from(across, along):
-        return ((chip // ring + across) % 2) * ring + (chip % ring + ring - along) % ring
+        return lax.rem(chip_across + across, 2) * ring + lax.rem(chip_along + ring - along, ring)
 
     def offset(t, size):
-        across = (t + 1) % 2
-        turn = t // 2
-        return across, (across * (1 + turn) + (1 - across) * (size - 1 - turn)) % size
+        if isinstance(t, int):
+            across, turn = (t + 1) % 2, t // 2
+            return across, (1 + turn if across else size - 1 - turn) % size
+        across, turn = lax.rem(t + 1, 2), lax.div(t, 2)
+        return across, lax.rem(across * (1 + turn) + (1 - across) * (size - 1 - turn), size)
 
     row_steps = [
         (far, step) for step in range(half_rows) for far in range(2) if (far, step) != (0, 0)
@@ -162,7 +169,7 @@
             greet(row_at(far, step), far_rep)
             greeted += 1
     for step in range(1, reps_n):
-        greet(row, (rep + step) % reps_n)
+        greet(row, lax.rem(rep + step, reps_n))
         greeted += 1
 
     inputs = [
@@ -171,6 +178,8 @@
             (
                 (features.at[share_rows(rep), :], feat_v.at[0]),
                 (features.at[share_rows(far_rep), :], feat_v.at[1]),
+                (live_hbm, live),
+                (column_hbm, column),
                 (self_weight, sw_v),
                 (neigh_weight, nw_v),
                 (bias, bias_v),
@@ -179,15 +188,11 @@
             )
         )
     ]
-    inputs[0].start()
-    inputs[1].start()
-    for block in range(BUFFERS):
-        mask_copy(block, block).start()
-    for copy in inputs[2:]:
+    for copy in inputs[:4]:
         copy.start()
 
     def expand(block, carry):
-        slot = block % BUFFERS
+        slot = lax.rem(block, BUFFERS)
         mask_copy(block, slot).wait()
         at = pl.ds(pl.multiple_of(block * tile, tile), tile)
         for s in range(rows_n):
@@ -214,14 +219,17 @@
             far_rep if far else rep,
         )
 
-    lax.fori_loop(0, blocks // 2, expand, 0)
-    inputs[0].wait()
-    inputs[1].wait()
+    for copy in inputs[:4]:
+        copy.wait()
     pl.semaphore_wait(barrier, greeted)
     for far, step in row_steps:
         feature_copy(0, far, step).start()
-    lax.fori_loop(blocks // 2, blocks, expand, 0)
-    for copy in inputs[2:]:
+    for block in range(BUFFERS):
+        mask_copy(block, block).start()
+    for copy in inputs[4:]:
+        copy.start()
+    lax.fori_loop(0, blocks, expand, 0)
+    for copy in inputs[4:]:
         copy.wait()
     for part in range(2):
         gathered[part, share_rows(row), :] = feat_v[0, :, part * half : (part + 1) * half]
@@ -256,30 +264,32 @@
 
     def finish_pair(part, t):
         pair_copy(part, t).wait_recv()
-        part_send[part, t] = (work[t % 2, core] + pair_recv[part, t].astype(F32)).astype(BF)
+        part_send[part, t] = (work[t % 4 if isinstance(t, int) else lax.rem(t, 4), core] + pair_recv[part, t].astype(F32)).astype(BF)
         part_copy(part, t).start()
 
     def forward(part):
         def body(t, carry):
             at = chip_at(*offset(t, ring))
             rows = pl.ds(pl.multiple_of(at * (2 * share), 2 * share), 2 * share)
-            work[t % 2] = jnp.dot(
+            work[lax.rem(t, 4)] = jnp.dot(
                 dense[rows, :], gathered[part], preferred_element_type=F32
             ).reshape(2, share, half)
-            pair_send[part, t] = work[t % 2, 1 - core].astype(BF)
+            pair_send[part, t] = work[lax.rem(t, 4), 1 - core].astype(BF)
             pair_copy(part, t).start()
 
-            @pl.when(t > 0)
+            @pl.when(t >= LAG)
             def _():
-                finish_pair(part, t - 1)
+                finish_pair(part, t - LAG)
 
             return carry
 
         for far, step in row_steps:
             feature_copy(part, far, step).wait_recv()
         lax.fori_loop(0, chips, body, 0)
+        for t in range(max(chips - LAG, 0), chips - 1):
+            finish_pair(part, t)
         pair_copy(part, chips - 1).wait_recv()
-        own_sum[part] = work[(chips - 1) % 2, core] + pair_recv[part, chips - 1].astype(F32)
+        own_sum[part] = work[(chips - 1) % 4, core] + pair_recv[part, chips - 1].astype(F32)
 
     forward(0)
     forward(1)
@@ -414,7 +424,7 @@
             rep,
         )
 
-    def backward(part):
+    def backward(part, low, high):
         def body(t, carry):
             target = row_at(*offset(t, half_rows))
             columns = pl.ds(pl.multiple_of(target * slot_width, slot_width), slot_width)
@@ -431,15 +441,12 @@
 
             return carry
 
-        lax.fori_loop(0, rows_n, body, 0)
+        lax.fori_loop(low, high, body, 0)
 
     relay_messages(0)
     finish_messages(0)
-    send_messages(1)
-    backward(0)
-
     def g2_copy(step):
-        to_rep = (rep + step) % reps_n
+        to_rep = lax.rem(rep + step, reps_n)
         return remote(g2_send.at[to_rep], g2_recv.at[step], sg2.at[step], rg2.at[step], row, to_rep)
 
     def g3_copy(far, step):
@@ -455,7 +462,8 @@
         source = chip_from(*offset(t, ring)) * 2 + core
         return remote(g4.at[source], g4.at[source], sg4f.at[t], rg4f.at[t], row, sibling)
 
-    relay_messages(1)
+    send_messages(1)
+    backward(0, 0, rows_n // 2)
     total = g1_send[row]
     for far, step in row_steps:
         g1_copy(far, step).wait_recv()
@@ -467,10 +475,8 @@
         g2_send[index, 2] = g1_sum[reps_n + 1]
     for step in range(1, reps_n):
         g2_copy(step).start()
-
-    finish_messages(1)
-    backward(1)
-
+    relay_messages(1)
+    backward(0, rows_n // 2, rows_n)
     total = g2_send[rep]
     for step in range(1, reps_n):
         g2_copy(step).wait_recv()
@@ -481,6 +487,15 @@
     for side in range(2):
         gb_v[:, side * half : (side + 1) * half] = total[1 + side][0:1, :]
     outs[3].start()
+    finish_messages(1)
+    backward(1, 0, rows_n // 2)
+    for far, step in row_steps:
+        g3_copy(far, step).wait_recv()
+    for t in range(chips - 1):
+        g4_copy(t).start()
+    g4[rep] = g3[...]
+    g4_pair(chips - 1).start()
+    backward(1, rows_n // 2, rows_n)
 
     def column_sums(part):
         total = direct[part] + back_own[part]
@@ -490,12 +505,6 @@
         gf_v[:, part * half : (part + 1) * half] = jnp.transpose(total).astype(BF)
 
     column_sums(0)
-    for far, step in row_steps:
-        g3_copy(far, step).wait_recv()
-    for t in range(chips - 1):
-        g4_copy(t).start()
-    g4[rep] = g3[...]
-    g4_pair(chips - 1).start()
     for t in range(chips - 1):
         g4_copy(t).wait_recv()
         g4_pair(t).start()
@@ -540,15 +549,23 @@
 
 
 def store(*refs):
-    count = len(refs) // 2
-    sems = refs[-1]
-    copies = [
-        pltpu.make_async_copy(refs[index], refs[count + index], sems.at[index])
+    count = (len(refs) - 2) // 3
+    given, results, staged = refs[:count], refs[count : 2 * count], refs[2 * count : 3 * count]
+    arrived, left = refs[3 * count :]
+    inward = [
+        pltpu.make_async_copy(given[index], staged[index], arrived.at[index])
         for index in range(count)
     ]
-    for copy in copies:
+    outward = [
+        pltpu.make_async_copy(staged[index], results[index], left.at[index])
+        for index in range(count)
+    ]
+    for copy in inward:
         copy.start()
-    for copy in copies:
+    for index in range(count):
+        inward[index].wait()
+        outward[index].start()
+    for copy in outward:
         copy.wait()
 
 
@@ -575,13 +592,14 @@
     scale = 1.0 / math.sqrt(share * rows_n * reps_n)
     block = (share, width)
     anywhere = pl.BlockSpec(memory_space=pl.ANY)
-    scalars = pl.BlockSpec(memory_space=pltpu.SMEM)
     dma = pltpu.SemaphoreType.DMA
     vmem = pltpu.VMEM
     grads = (reps_n + 2, tile_rows, lanes)
     half_block = (share, lanes)
     turned = (lanes, share)
     scratch = [
+        pltpu.SMEM((slots, panel_rows // tile), jnp.int32),
+        pltpu.SMEM((slots, panel_rows // tile), jnp.int32),
         vmem((panel_rows, slots * share), BF),
         vmem((BUFFERS, tile * slots, tile), jnp.int32),
         vmem((2, *block), BF),
@@ -591,7 +609,7 @@
         vmem((1, width), F32),
         vmem((1, share), jnp.int32),
         vmem(block, BF),
-        vmem((2, 2, *half_block), F32),
+        vmem((4, 2, *half_block), F32),
         vmem((2, chips, *half_block), BF),
         vmem((2, chips, *half_block), BF),
         vmem((2, chips, *half_block), BF),
@@ -617,7 +635,7 @@
         vmem((width, width), F32),
         vmem((1, width), F32),
         dma((BUFFERS,)),
-        dma((7,)),
+        dma((9,)),
         dma((5,)),
         dma((2, rows_n)),
         dma((2, rows_n)),
@@ -633,7 +651,7 @@
             jax.ShapeDtypeStruct((width, width), F32),
             jax.ShapeDtypeStruct((1, width), F32),
         ),
-        in_specs=[anywhere] * 5 + [scalars] * 2 + [anywhere] * 2,
+        in_specs=[anywhere] * 9,
         out_specs=(anywhere,) * 5,
         scratch_shapes=scratch,
         compiler_params=pltpu.CompilerParams(
@@ -656,7 +674,7 @@
         out_shape=tuple(jax.ShapeDtypeStruct(one.shape, one.dtype) for one in results),
         in_specs=[anywhere] * 5,
         out_specs=(anywhere,) * 5,
-        scratch_shapes=[dma((5,))],
+        scratch_shapes=[vmem(one.shape, one.dtype) for one in results] + [dma((5,))] * 2,
         name="store",
     )(*results)
     return (hidden, grad_features, grad_self, grad_neigh, grad_bias.reshape(width))

time: 105 us -> 74.5 us (0.71)
  Pallas kernels: 104 us -> 73.7 us
    pallas_call x1, Pallas kernels: 25 us -> 1.96 us  [per_device(): pl.pallas_call(store, out_shape=tuple((jax.ShapeDtypeStruct(one.shape, on...]
    pallas_call x1, Pallas kernels: 78.8 us -> 71.7 us  [per_device(): pl.pallas_call(functools.partial(kernel, rows_n, reps_n, scale), out_shap...]
where the time goes in v3:
time: 74.5 us; the launch traced here: 74.3 us
  Pallas kernels  73.7 us (99%)
    pallas_call x1, Pallas kernels, per_device(): pl.pallas_call(functools.partial(kernel, rows_n, reps_n, scale), out_shap...  71.7 us
    pallas_call x1, Pallas kernels, per_device(): pl.pallas_call(store, out_shape=tuple((jax.ShapeDtypeStruct(one.shape, on...  1.96 us

profile of v3, /device:TPU:1, one launch (start us, length us, event | category | flops | bytes accessed | tf_op | source)
XLA Modules:
  0.0 74.3 jit_solution(13545370010589950870)
XLA Ops:
  0.6 71.7 %layer.1 = (bf16[256,256]{1,0:T(8,128)(2,1)}, bf16[256,256]{1,0:T(8,128)(2,1)}, f32[256,256]{1,0:T(8,128)}, f32[256,256]{1,0:T(8,128)}, f32[1,256]{1,0:T(1,128)}) custom-call(bf16[4096,256]{1,0:T(8,128)(2,1)} %features.1, bf16[256,256]{1,0:T(8,128)(2,1)} %self_weight.1, bf16[256,256]{1,0:T(8,128)(2,1)} %neigh_weight.1, f32[1,256]{1,0:T(1,128)} %bitcast.9, ...), custom_call_target="tpu_custom_call" | custom-call | tf_op jit(solution)/shard_map/layer/pallas_call | solution.py:645
  72.4 2.0 %store.1 = (bf16[256,256]{1,0:T(8,128)(2,1)}, bf16[256,256]{1,0:T(8,128)(2,1)}, f32[256,256]{1,0:T(8,128)}, f32[256,256]{1,0:T(8,128)}, f32[1,256]{1,0:T(1,128)}) custom-call(bf16[256,256]{1,0:T(8,128)(2,1)} %get-tuple-element.15.refs_0_, bf16[256,256]{1,0:T(8,128)(2,1)} %get-tuple-element.16.refs_1_, f32[256,256]{1,0:T(8,128)} %get-tuple-element.17.refs_2_, ...), custom_call_target="tpu_custom_call" | custom-call | tf_op jit(solution)/shard_map/store/pallas_call | solution.py:672

commit v4 on v3

--- a/solution.py
+++ b/solution.py
@@ -29,11 +29,11 @@
     column_hbm,
     degree,
     cotangent,
-    hidden_out,
-    grad_features,
-    grad_self,
-    grad_neigh,
-    grad_bias,
+    hid_v,
+    gf_v,
+    gs_v,
+    gn_v,
+    gb_v,
     live,
     column,
     dense,
@@ -65,14 +65,8 @@
     g2_recv,
     g3,
     g4,
-    hid_v,
-    gf_v,
-    gs_v,
-    gn_v,
-    gb_v,
     mask_sem,
     in_sem,
-    out_sem,
     s1,
     r1,
     s2p,
@@ -228,7 +222,13 @@
         mask_copy(block, block).start()
     for copy in inputs[4:]:
         copy.start()
-    lax.fori_loop(0, blocks, expand, 0)
+    early = blocks - blocks // 5
+    lax.fori_loop(0, early, expand, 0)
+    for far, step in row_steps:
+        feature_copy(0, far, step).wait_send()
+    for far, step in row_steps:
+        feature_copy(1, far, step).start()
+    lax.fori_loop(early, blocks, expand, 0)
     for copy in inputs[4:]:
         copy.wait()
     for part in range(2):
@@ -237,10 +237,6 @@
     pre_v[...] = jnp.dot(own, sw_v[...], preferred_element_type=F32) + bias_v[...]
     degree_row = degree_v[...].astype(F32)
     degree_column = jnp.transpose(jnp.broadcast_to(degree_row, (half, share)))
-    for far, step in row_steps:
-        feature_copy(0, far, step).wait_send()
-    for far, step in row_steps:
-        feature_copy(1, far, step).start()
 
     def pair_copy(part, t):
         return remote(
@@ -315,7 +311,7 @@
     dpre_b = dpre.astype(BF)
 
     def message_copy(part, across, along):
-        relay = across and along
+        relay = relayed(part, across, along)
         source = (chip_at(1, 0) if relay else chip) * 2 + core
         place = msg_all.at[part, :, share_rows(source)]
         index = across * ring + along
@@ -329,17 +325,17 @@
 
     along_order = sorted(range(1, ring), key=lambda d: min(d, ring - d))
 
-    def send_messages(part):
-        message_copy(part, 1, 0).start()
-        for along in along_order:
-            message_copy(part, 0, along).start()
-        sibling_copy(part, 0, 0).start()
-
-    def relay_messages(part):
-        message_copy(part, 1, 0).wait_recv()
-        for along in along_order:
-            message_copy(part, 1, along).start()
-        sibling_copy(part, 1, 0).start()
+    def relayed(part, across, along):
+        return across == 1 and along > 0 and (part == 1 or along == ring // 2)
+
+    own_first = [(1, 0)] + [
+        (across, along)
+        for along in along_order
+        for across in range(2)
+        if not relayed(0, across, along)
+    ]
+    relay_first = [(1, along) for along in along_order if relayed(0, 1, along)]
+    all_second = [(across, along) for along in along_order for across in range(2)]
 
     def finish_messages(part):
         for across in range(2):
@@ -361,22 +357,14 @@
             / degree_row
         ).astype(BF)
         if part == 0:
-            send_messages(0)
-
-    outs = [
-        pltpu.make_async_copy(src, dst, out_sem.at[index])
-        for index, (src, dst) in enumerate(
-            (
-                (hid_v, hidden_out),
-                (gs_v, grad_self),
-                (gn_v, grad_neigh),
-                (gb_v, grad_bias),
-                (gf_v, grad_features),
-            )
-        )
-    ]
+            for offsets in own_first:
+                message_copy(0, *offsets).start()
+            sibling_copy(0, 0, 0).start()
+        else:
+            message_copy(1, 1, 0).start()
+            sibling_copy(1, 0, 0).start()
+
     hid_v[...] = (0.5 * pre * (1.0 + bend)).astype(BF)
-    outs[0].start()
 
     g_rows = 2 * width // rows_n
     tile_rows = g_rows // (reps_n // 2)
@@ -443,7 +431,16 @@
 
         lax.fori_loop(low, high, body, 0)
 
-    relay_messages(0)
+    message_copy(0, 1, 0).wait_recv()
+    for offsets in relay_first:
+        message_copy(0, *offsets).start()
+    sibling_copy(0, 1, 0).start()
+    for offsets in own_first:
+        message_copy(0, *offsets).wait_send()
+    message_copy(1, 1, 0).wait_recv()
+    for offsets in all_second:
+        message_copy(1, *offsets).start()
+    sibling_copy(1, 1, 0).start()
     finish_messages(0)
     def g2_copy(step):
         to_rep = lax.rem(rep + step, reps_n)
@@ -462,8 +459,7 @@
         source = chip_from(*offset(t, ring)) * 2 + core
         return remote(g4.at[source], g4.at[source], sg4f.at[t], rg4f.at[t], row, sibling)
 
-    send_messages(1)
-    backward(0, 0, rows_n // 2)
+    backward(0, 0, rows_n // 4)
     total = g1_send[row]
     for far, step in row_steps:
         g1_copy(far, step).wait_recv()
@@ -475,8 +471,7 @@
         g2_send[index, 2] = g1_sum[reps_n + 1]
     for step in range(1, reps_n):
         g2_copy(step).start()
-    relay_messages(1)
-    backward(0, rows_n // 2, rows_n)
+    backward(0, rows_n // 4, rows_n)
     total = g2_send[rep]
     for step in range(1, reps_n):
         g2_copy(step).wait_recv()
@@ -486,7 +481,6 @@
         g3_copy(far, step).start()
     for side in range(2):
         gb_v[:, side * half : (side + 1) * half] = total[1 + side][0:1, :]
-    outs[3].start()
     finish_messages(1)
     backward(1, 0, rows_n // 2)
     for far, step in row_steps:
@@ -517,10 +511,7 @@
             out[low : low + g_rows, side * half : (side + 1) * half] = g4[
                 side * (reps_n // 2) : (side + 1) * (reps_n // 2), index
             ].reshape(g_rows, half)
-    outs[1].start()
-    outs[2].start()
     column_sums(1)
-    outs[4].start()
 
     for far, step in row_steps:
         feature_copy(1, far, step).wait_send()
@@ -535,7 +526,7 @@
             back_copy(part, t).wait_send()
         for across in range(2):
             for along in range(ring):
-                if across or along:
+                if (across or along) and not (part == 0 and (across, along) in own_first):
                     message_copy(part, across, along).wait_send()
                 sibling_copy(part, across, along).wait_send()
     for step in range(1, reps_n):
@@ -544,28 +535,18 @@
         if t < chips - 1:
             g4_copy(t).wait_send()
         g4_pair(t).wait_send()
-    for copy in outs:
-        copy.wait()
 
 
 def store(*refs):
-    count = (len(refs) - 2) // 3
-    given, results, staged = refs[:count], refs[count : 2 * count], refs[2 * count : 3 * count]
-    arrived, left = refs[3 * count :]
-    inward = [
-        pltpu.make_async_copy(given[index], staged[index], arrived.at[index])
+    count = len(refs) // 2
+    sems = refs[-1]
+    copies = [
+        pltpu.make_async_copy(refs[index], refs[count + index], sems.at[index])
         for index in range(count)
     ]
-    outward = [
-        pltpu.make_async_copy(staged[index], results[index], left.at[index])
-        for index in range(count)
-    ]
-    for copy in inward:
+    for copy in copies:
         copy.start()
-    for index in range(count):
-        inward[index].wait()
-        outward[index].start()
-    for copy in outward:
+    for copy in copies:
         copy.wait()
 
 
@@ -629,14 +610,8 @@
         vmem((reps_n, 3, tile_rows, lanes), F32),
         vmem((rows_n, tile_rows, lanes), F32),
         vmem((reps_n, rows_n, tile_rows, lanes), F32),
-        vmem(block, BF),
-        vmem(block, BF),
-        vmem((width, width), F32),
-        vmem((width, width), F32),
-        vmem((1, width), F32),
         dma((BUFFERS,)),
         dma((9,)),
-        dma((5,)),
         dma((2, rows_n)),
         dma((2, rows_n)),
     ]
@@ -645,14 +620,14 @@
     results = pl.pallas_call(
         functools.partial(kernel, rows_n, reps_n, scale),
         out_shape=(
-            jax.ShapeDtypeStruct(block, BF),
-            jax.ShapeDtypeStruct(block, BF),
-            jax.ShapeDtypeStruct((width, width), F32),
-            jax.ShapeDtypeStruct((width, width), F32),
-            jax.ShapeDtypeStruct((1, width), F32),
+            vmem(block, BF),
+            vmem(block, BF),
+            vmem((width, width), F32),
+            vmem((width, width), F32),
+            vmem((1, width), F32),
         ),
         in_specs=[anywhere] * 9,
-        out_specs=(anywhere,) * 5,
+        out_specs=(pl.BlockSpec(memory_space=vmem),) * 5,
         scratch_shapes=scratch,
         compiler_params=pltpu.CompilerParams(
             collective_id=0, has_side_effects=True, vmem_limit_bytes=56 * 1024 * 1024
@@ -672,11 +647,11 @@
     hidden, grad_features, grad_self, grad_neigh, grad_bias = pl.pallas_call(
         store,
         out_shape=tuple(jax.ShapeDtypeStruct(one.shape, one.dtype) for one in results),
-        in_specs=[anywhere] * 5,
+        in_specs=[pl.BlockSpec(memory_space=vmem)] * 5,
         out_specs=(anywhere,) * 5,
-        scratch_shapes=[vmem(one.shape, one.dtype) for one in results] + [dma((5,))] * 2,
+        scratch_shapes=[dma((5,))],
         name="store",
-    )(*results)
+    )(*[pltpu.with_memory_space_constraint(one, vmem) for one in results])
     return (hidden, grad_features, grad_self, grad_neigh, grad_bias.reshape(width))
 
 

time: 74.5 us -> 70.8 us (0.950)
  Pallas kernels: 73.7 us -> 70 us
    pallas_call x1, Pallas kernels: 71.7 us -> 69.1 us  [per_device(): pl.pallas_call(functools.partial(kernel, rows_n, reps_n, scale), out_shap...]
    pallas_call x1, Pallas kernels: 1.96 us -> 0.92 us  [per_device(): pl.pallas_call(store, out_shape=tuple((jax.ShapeDtypeStruct(one.shape, on...]
where the time goes in v4:
time: 70.8 us; the launch traced here: 70.6 us
  Pallas kernels  70 us (99%)
    pallas_call x1, Pallas kernels, per_device(): pl.pallas_call(functools.partial(kernel, rows_n, reps_n, scale), out_shap...  69.1 us

profile of v4, /device:TPU:1, one launch (start us, length us, event | category | flops | bytes accessed | tf_op | source)
XLA Modules:
  0.0 70.6 jit_solution(8017781629174902123)
XLA Ops:
  0.6 69.1 %layer.1 = (bf16[256,256]{1,0:T(8,128)(2,1)S(1)}, bf16[256,256]{1,0:T(8,128)(2,1)S(1)}, f32[256,256]{1,0:T(8,128)S(1)}, f32[256,256]{1,0:T(8,128)S(1)}, f32[1,256]{1,0:T(1,128)S(1)}) custom-call(bf16[4096,256]{1,0:T(8,128)(2,1)} %features.1, bf16[256,256]{1,0:T(8,128)(2,1)} %self_weight.1, bf16[256,256]{1,0:T(8,128)(2,1)} %neigh_weight.1, f32[1,256]{1,0:T(1,128)} %bitcast.9, ...), custom_call_target="tpu_custom_call" | custom-call | tf_op jit(solution)/shard_map/layer/pallas_call | solution.py:620
  69.7 0.9 %store.1 = (bf16[256,256]{1,0:T(8,128)(2,1)}, bf16[256,256]{1,0:T(8,128)(2,1)}, f32[256,256]{1,0:T(8,128)}, f32[256,256]{1,0:T(8,128)}, f32[1,256]{1,0:T(1,128)}) custom-call(bf16[256,256]{1,0:T(8,128)(2,1)S(1)} %get-tuple-element.15.refs_0_, bf16[256,256]{1,0:T(8,128)(2,1)S(1)} %get-tuple-element.16.refs_1_, f32[256,256]{1,0:T(8,128)S(1)} %get-tuple-element.17.refs_2_, ...), custom_call_target="tpu_custom_call" | custom-call | tf_op jit(solution)/shard_map/store/pallas_call | solution.py:647

commit v5 on v4

--- a/solution.py
+++ b/solution.py
@@ -58,6 +58,8 @@
     back_own,
     back_send,
     back_recv,
+    g_term,
+    g_pair,
     g1_send,
     g1_recv,
     g1_sum,
@@ -79,6 +81,8 @@
     r3f,
     s4,
     r4,
+    sg0,
+    rg0,
     sg1,
     rg1,
     sg2,
@@ -366,23 +370,22 @@
 
     hid_v[...] = (0.5 * pre * (1.0 + bend)).astype(BF)
 
-    g_rows = 2 * width // rows_n
-    tile_rows = g_rows // (reps_n // 2)
-    terms = [
-        lax.dot_general(left, dpre_b, CONTRACT_FIRST, preferred_element_type=F32) * scale
-        for left in (feat_v[0], mean_v[...])
-    ]
-    bias_term = jnp.sum(dpre, axis=0, keepdims=True) * scale
-    for index in range(rows_n):
-        term = terms[index * g_rows // width]
-        low = index * g_rows % width
-        for side in range(2):
-            g1_send[index, side * (reps_n // 2) : (side + 1) * (reps_n // 2)] = term[
-                low : low + g_rows, side * half : (side + 1) * half
-            ].reshape(reps_n // 2, tile_rows, half)
-            g1_send[index, reps_n + side] = jnp.broadcast_to(
-                bias_term[:, side * half : (side + 1) * half], (tile_rows, half)
-            )
+    g_rows = width // rows_n
+    tile_rows = g_rows // (chips // 2)
+    bias_term = jnp.broadcast_to(jnp.sum(dpre, axis=0, keepdims=True) * scale, (8, width))
+    for index, left in enumerate((feat_v[0], mean_v[...])):
+        g_term[index, :width, :] = (
+            lax.dot_general(left, dpre_b, CONTRACT_FIRST, preferred_element_type=F32) * scale
+        )
+        g_term[index, width:, :] = bias_term
+
+    def g0_copy():
+        return remote(g_term.at[1 - core], g_pair, sg0.at[0], rg0.at[0], row, sibling)
+
+    g0_copy().start()
+    direct[...] = lax.dot_general(
+        sw_v[...], dpre_b, CONTRACT_LAST, preferred_element_type=F32
+    ).reshape(2, half, share)
 
     def g1_copy(far, step):
         index = far * half_rows + step
@@ -396,12 +399,6 @@
             far_rep if far else rep,
         )
 
-    for far, step in row_steps:
-        g1_copy(far, step).start()
-    direct[...] = lax.dot_general(
-        sw_v[...], dpre_b, CONTRACT_LAST, preferred_element_type=F32
-    ).reshape(2, half, share)
-
     def back_copy(part, t):
         return remote(
             back_send.at[part, t],
@@ -435,6 +432,18 @@
     for offsets in relay_first:
         message_copy(0, *offsets).start()
     sibling_copy(0, 1, 0).start()
+    g0_copy().wait_recv()
+    summed = g_term[core] + g_pair[...]
+    for index in range(rows_n):
+        for side in range(2):
+            g1_send[index, side * (chips // 2) : (side + 1) * (chips // 2)] = summed[
+                index * g_rows : (index + 1) * g_rows, side * half : (side + 1) * half
+            ].reshape(chips // 2, tile_rows, half)
+            g1_send[index, chips + side] = jnp.broadcast_to(
+                summed[width : width + 1, side * half : (side + 1) * half], (tile_rows, half)
+            )
+    for far, step in row_steps:
+        g1_copy(far, step).start()
     for offsets in own_first:
         message_copy(0, *offsets).wait_send()
     message_copy(1, 1, 0).wait_recv()
@@ -442,40 +451,40 @@
         message_copy(1, *offsets).start()
     sibling_copy(1, 1, 0).start()
     finish_messages(0)
-    def g2_copy(step):
-        to_rep = lax.rem(rep + step, reps_n)
-        return remote(g2_send.at[to_rep], g2_recv.at[step], sg2.at[step], rg2.at[step], row, to_rep)
+    def g2_copy(t):
+        to_chip = chip_at(*offset(t, ring))
+        return remote(
+            g2_send.at[to_chip], g2_recv.at[t], sg2.at[t], rg2.at[t], row, to_chip * 2 + core
+        )
 
     def g3_copy(far, step):
         index = far * half_rows + step
         return remote(g3.at[row], g3.at[row], sg3.at[index], rg3.at[index], row_at(far, step), rep)
 
     def g4_copy(t):
-        return remote(
-            g3, g4.at[rep], sg4.at[t], rg4.at[t], row, chip_at(*offset(t, ring)) * 2 + core
-        )
+        to_rep = chip_at(*offset(t, ring)) * 2 + core
+        return remote(g3, g4.at[core, chip], sg4.at[t], rg4.at[t], row, to_rep)
 
     def g4_pair(t):
-        source = chip_from(*offset(t, ring)) * 2 + core
-        return remote(g4.at[source], g4.at[source], sg4f.at[t], rg4f.at[t], row, sibling)
-
-    backward(0, 0, rows_n // 4)
+        place = g4.at[core, chip_from(*offset(t, ring))]
+        return remote(place, place, sg4f.at[t], rg4f.at[t], row, sibling)
+
     total = g1_send[row]
     for far, step in row_steps:
         g1_copy(far, step).wait_recv()
         total = total + g1_recv[far * half_rows + step]
     g1_sum[...] = total
-    for index in range(reps_n):
+    for index in range(chips):
         g2_send[index, 0] = g1_sum[index]
-        g2_send[index, 1] = g1_sum[reps_n]
-        g2_send[index, 2] = g1_sum[reps_n + 1]
-    for step in range(1, reps_n):
-        g2_copy(step).start()
-    backward(0, rows_n // 4, rows_n)
-    total = g2_send[rep]
-    for step in range(1, reps_n):
-        g2_copy(step).wait_recv()
-        total = total + g2_recv[step]
+        g2_send[index, 1] = g1_sum[chips]
+        g2_send[index, 2] = g1_sum[chips + 1]
+    for t in range(chips - 1):
+        g2_copy(t).start()
+    backward(0, 0, rows_n)
+    total = g2_send[chip]
+    for t in range(chips - 1):
+        g2_copy(t).wait_recv()
+        total = total + g2_recv[t]
     g3[row] = total[0]
     for far, step in row_steps:
         g3_copy(far, step).start()
@@ -487,7 +496,7 @@
         g3_copy(far, step).wait_recv()
     for t in range(chips - 1):
         g4_copy(t).start()
-    g4[rep] = g3[...]
+    g4[core, chip] = g3[...]
     g4_pair(chips - 1).start()
     backward(1, rows_n // 2, rows_n)
 
@@ -504,13 +513,14 @@
         g4_pair(t).start()
     for t in range(chips):
         g4_pair(t).wait_recv()
-    for index in range(rows_n):
-        out = (gs_v, gn_v)[index * g_rows // width]
-        low = index * g_rows % width
-        for side in range(2):
-            out[low : low + g_rows, side * half : (side + 1) * half] = g4[
-                side * (reps_n // 2) : (side + 1) * (reps_n // 2), index
-            ].reshape(g_rows, half)
+    for index, out in enumerate((gs_v, gn_v)):
+        for place in range(rows_n):
+            for side in range(2):
+                out[
+                    place * g_rows : (place + 1) * g_rows, side * half : (side + 1) * half
+                ] = g4[index, side * (chips // 2) : (side + 1) * (chips // 2), place].reshape(
+                    g_rows, half
+                )
     column_sums(1)
 
     for far, step in row_steps:
@@ -529,10 +539,10 @@
                 if (across or along) and not (part == 0 and (across, along) in own_first):
                     message_copy(part, across, along).wait_send()
                 sibling_copy(part, across, along).wait_send()
-    for step in range(1, reps_n):
-        g2_copy(step).wait_send()
+    g0_copy().wait_send()
     for t in range(chips):
         if t < chips - 1:
+            g2_copy(t).wait_send()
             g4_copy(t).wait_send()
         g4_pair(t).wait_send()
 
@@ -569,13 +579,13 @@
     tile = tile_masks.shape[2]
     chips = reps_n // 2
     lanes = width // 2
-    tile_rows = 2 * width // rows_n // (reps_n // 2)
+    tile_rows = width // rows_n // (chips // 2)
     scale = 1.0 / math.sqrt(share * rows_n * reps_n)
     block = (share, width)
     anywhere = pl.BlockSpec(memory_space=pl.ANY)
     dma = pltpu.SemaphoreType.DMA
     vmem = pltpu.VMEM
-    grads = (reps_n + 2, tile_rows, lanes)
+    grads = (chips + 2, tile_rows, lanes)
     half_block = (share, lanes)
     turned = (lanes, share)
     scratch = [
@@ -603,20 +613,22 @@
         vmem((2, *turned), F32),
         vmem((2, rows_n, *turned), BF),
         vmem((2, rows_n, *turned), BF),
+        vmem((2, width + 8, width), F32),
+        vmem((width + 8, width), F32),
         vmem((rows_n, *grads), F32),
         vmem((rows_n, *grads), F32),
         vmem(grads, F32),
-        vmem((reps_n, 3, tile_rows, lanes), F32),
-        vmem((reps_n, 3, tile_rows, lanes), F32),
+        vmem((chips, 3, tile_rows, lanes), F32),
+        vmem((chips, 3, tile_rows, lanes), F32),
         vmem((rows_n, tile_rows, lanes), F32),
-        vmem((reps_n, rows_n, tile_rows, lanes), F32),
+        vmem((2, chips, rows_n, tile_rows, lanes), F32),
         dma((BUFFERS,)),
         dma((9,)),
         dma((2, rows_n)),
         dma((2, rows_n)),
     ]
-    scratch += [dma((2, chips))] * 8 + [dma((2, rows_n))] * 2 + [dma((rows_n,))] * 2
-    scratch += [dma((reps_n,))] * 2 + [dma((rows_n,))] * 2 + [dma((chips,))] * 4
+    scratch += [dma((2, chips))] * 8 + [dma((2, rows_n))] * 2 + [dma((1,))] * 2 + [dma((rows_n,))] * 2
+    scratch += [dma((chips,))] * 2 + [dma((rows_n,))] * 2 + [dma((chips,))] * 4
     results = pl.pallas_call(
         functools.partial(kernel, rows_n, reps_n, scale),
         out_shape=(

time: 70.8 us -> 68.6 us (0.969)
  Pallas kernels: 70 us -> 67.8 us
    pallas_call x1, Pallas kernels: 69.1 us -> 66.9 us  [per_device(): pl.pallas_call(functools.partial(kernel, rows_n, reps_n, scale), out_shap...]
where the time goes in v5:
time: 68.6 us; the launch traced here: 68.5 us
  Pallas kernels  67.8 us (99%)
    pallas_call x1, Pallas kernels, per_device(): pl.pallas_call(functools.partial(kernel, rows_n, reps_n, scale), out_shap...  66.9 us

profile of v5, /device:TPU:1, one launch (start us, length us, event | category | flops | bytes accessed | tf_op | source)
XLA Modules:
  0.0 68.5 jit_solution(1278594088906415709)
XLA Ops:
  0.6 66.9 %layer.1 = (bf16[256,256]{1,0:T(8,128)(2,1)S(1)}, bf16[256,256]{1,0:T(8,128)(2,1)S(1)}, f32[256,256]{1,0:T(8,128)S(1)}, f32[256,256]{1,0:T(8,128)S(1)}, f32[1,256]{1,0:T(1,128)S(1)}) custom-call(bf16[4096,256]{1,0:T(8,128)(2,1)} %features.1, bf16[256,256]{1,0:T(8,128)(2,1)} %self_weight.1, bf16[256,256]{1,0:T(8,128)(2,1)} %neigh_weight.1, f32[1,256]{1,0:T(1,128)} %bitcast.9, ...), custom_call_target="tpu_custom_call" | custom-call | tf_op jit(solution)/shard_map/layer/pallas_call | solution.py:632
  67.5 0.9 %store.1 = (bf16[256,256]{1,0:T(8,128)(2,1)}, bf16[256,256]{1,0:T(8,128)(2,1)}, f32[256,256]{1,0:T(8,128)}, f32[256,256]{1,0:T(8,128)}, f32[1,256]{1,0:T(1,128)}) custom-call(bf16[256,256]{1,0:T(8,128)(2,1)S(1)} %get-tuple-element.15.refs_0_, bf16[256,256]{1,0:T(8,128)(2,1)S(1)} %get-tuple-element.16.refs_1_, f32[256,256]{1,0:T(8,128)S(1)} %get-tuple-element.17.refs_2_, ...), custom_call_target="tpu_custom_call" | custom-call | tf_op jit(solution)/shard_map/store/pallas_call | solution.py:659

commit v6 on v5

--- a/solution.py
+++ b/solution.py
@@ -142,9 +142,10 @@
         across, turn = lax.rem(t + 1, 2), lax.div(t, 2)
         return across, lax.rem(across * (1 + turn) + (1 - across) * (size - 1 - turn), size)
 
-    row_steps = [
-        (far, step) for step in range(half_rows) for far in range(2) if (far, step) != (0, 0)
-    ]
+    row_steps = sorted(
+        ((far, step) for step in range(half_rows) for far in range(2) if (far, step) != (0, 0)),
+        key=lambda at: (-min(at[1], half_rows - at[1]), -at[0]),
+    )
 
     def mask_copy(block, slot):
         return pltpu.make_async_copy(

time: 68.6 us -> 67.8 us (0.988)
  Pallas kernels: 67.8 us -> 67 us
    pallas_call x1, Pallas kernels: 66.9 us -> 66.1 us  [per_device(): pl.pallas_call(functools.partial(kernel, rows_n, reps_n, scale), out_shap...]
where the time goes in v6:
time: 67.8 us; the launch traced here: 67.7 us
  Pallas kernels  67 us (99%)
    pallas_call x1, Pallas kernels, per_device(): pl.pallas_call(functools.partial(kernel, rows_n, reps_n, scale), out_shap...  66.1 us

profile of v6, /device:TPU:1, one launch (start us, length us, event | category | flops | bytes accessed | tf_op | source)
XLA Modules:
  0.0 67.7 jit_solution(16426196315529307169)
XLA Ops:
  0.6 66.1 %layer.1 = (bf16[256,256]{1,0:T(8,128)(2,1)S(1)}, bf16[256,256]{1,0:T(8,128)(2,1)S(1)}, f32[256,256]{1,0:T(8,128)S(1)}, f32[256,256]{1,0:T(8,128)S(1)}, f32[1,256]{1,0:T(1,128)S(1)}) custom-call(bf16[4096,256]{1,0:T(8,128)(2,1)} %features.1, bf16[256,256]{1,0:T(8,128)(2,1)} %self_weight.1, bf16[256,256]{1,0:T(8,128)(2,1)} %neigh_weight.1, f32[1,256]{1,0:T(1,128)} %bitcast.9, ...), custom_call_target="tpu_custom_call" | custom-call | tf_op jit(solution)/shard_map/layer/pallas_call | solution.py:633
  66.7 0.9 %store.1 = (bf16[256,256]{1,0:T(8,128)(2,1)}, bf16[256,256]{1,0:T(8,128)(2,1)}, f32[256,256]{1,0:T(8,128)}, f32[256,256]{1,0:T(8,128)}, f32[1,256]{1,0:T(1,128)}) custom-call(bf16[256,256]{1,0:T(8,128)(2,1)S(1)} %get-tuple-element.15.refs_0_, bf16[256,256]{1,0:T(8,128)(2,1)S(1)} %get-tuple-element.16.refs_1_, f32[256,256]{1,0:T(8,128)S(1)} %get-tuple-element.17.refs_2_, ...), custom_call_target="tpu_custom_call" | custom-call | tf_op jit(solution)/shard_map/store/pallas_call | solution.py:660

commit v7 on v6

--- a/solution.py
+++ b/solution.py
@@ -339,6 +339,7 @@
         for across in range(2)
         if not relayed(0, across, along)
     ]
+    own_first.sort(key=lambda at: -2 * (at == (1, 0)) - (at[0] + min(at[1], ring - at[1]) > 1))
     relay_first = [(1, along) for along in along_order if relayed(0, 1, along)]
     all_second = [(across, along) for along in along_order for across in range(2)]
 

time: 67.8 us -> 67.8 us (level)
  no operation moved by 1% of the time
where the time goes in v7:
time: 67.8 us; the launch traced here: 67.7 us
  Pallas kernels  67 us (99%)
    pallas_call x1, Pallas kernels, per_device(): pl.pallas_call(functools.partial(kernel, rows_n, reps_n, scale), out_shap...  66.1 us

profile of v7, /device:TPU:1, one launch (start us, length us, event | category | flops | bytes accessed | tf_op | source)
XLA Modules:
  0.0 67.7 jit_solution(2048843100424749687)
XLA Ops:
  0.6 66.1 %layer.1 = (bf16[256,256]{1,0:T(8,128)(2,1)S(1)}, bf16[256,256]{1,0:T(8,128)(2,1)S(1)}, f32[256,256]{1,0:T(8,128)S(1)}, f32[256,256]{1,0:T(8,128)S(1)}, f32[1,256]{1,0:T(1,128)S(1)}) custom-call(bf16[4096,256]{1,0:T(8,128)(2,1)} %features.1, bf16[256,256]{1,0:T(8,128)(2,1)} %self_weight.1, bf16[256,256]{1,0:T(8,128)(2,1)} %neigh_weight.1, f32[1,256]{1,0:T(1,128)} %bitcast.9, ...), custom_call_target="tpu_custom_call" | custom-call | tf_op jit(solution)/shard_map/layer/pallas_call | solution.py:634
  66.7 0.9 %store.1 = (bf16[256,256]{1,0:T(8,128)(2,1)}, bf16[256,256]{1,0:T(8,128)(2,1)}, f32[256,256]{1,0:T(8,128)}, f32[256,256]{1,0:T(8,128)}, f32[1,256]{1,0:T(1,128)}) custom-call(bf16[256,256]{1,0:T(8,128)(2,1)S(1)} %get-tuple-element.15.refs_0_, bf16[256,256]{1,0:T(8,128)(2,1)S(1)} %get-tuple-element.16.refs_1_, f32[256,256]{1,0:T(8,128)S(1)} %get-tuple-element.17.refs_2_, ...), custom_call_target="tpu_custom_call" | custom-call | tf_op jit(solution)/shard_map/store/pallas_call | solution.py:661
